TPU v7x, 128 devices: a whole 4x4x4 slice. The times are simulated.
128 devices in a mesh: req: 8 (over x, y_hi), mdl: 16 (over z, y_lo, core).
Axes of the slice: x: 4, y: 4 (y_hi: 2, y_lo: 2; y = y_hi * 2 + y_lo), z: 4, core: 2. Of those that a mesh axis runs over, the one named last changes fastest.
Arguments:
- tokens: bfloat16 [16384, 1536], P(('req', 'mdl')), may hold values from -3 to 3
- attention_gain: bfloat16 [1536], replicated, may hold values from 0.099609375 to 1.8984375
- feed_gain: bfloat16 [1536], replicated, may hold values from 0.099609375 to 1.8984375
- w_query: bfloat16 [1536, 1536], P('req', 'mdl'), may hold values from -0.4375 to 0.4375
- w_key: bfloat16 [1536, 768], P('req', 'mdl'), may hold values from -0.15625 to 0.15625
- w_value: bfloat16 [1536, 768], P('req', 'mdl'), may hold values from -0.15625 to 0.15625
- w_out: bfloat16 [1536, 1536], P('mdl', 'req'), may hold values from -0.15625 to 0.15625
- w_gate: bfloat16 [1536, 4096], P('req', 'mdl'), may hold values from -0.15625 to 0.15625
- w_up: bfloat16 [1536, 4096], P('req', 'mdl'), may hold values from -0.15625 to 0.15625
- w_down: bfloat16 [4096, 1536], P('mdl', 'req'), may hold values from -0.09375 to 0.09375
- prefix_cache: bfloat16 [2, 8, 4096, 768], P(None, 'req', None, 'mdl'), may hold values from -400 to 400
- lengths: int32 [32], replicated, may hold values from 0 to 512, as said below
- member: int32 [32], replicated, may hold values from 0 to 7
- owners: int32 [8], replicated, may hold values from 0 to 7, as said below
Outputs:
- hidden: bfloat16 [16384, 1536], P(('req', 'mdl'))
- suffix_cache: bfloat16 [2, 16384, 768], P(None, 'req', 'mdl')
Inputs may be any that keep to these rules, and one draw needn't show every extreme that they name: `lengths`: some request has 512 live tokens in every draw. Request r reads the prefix of group member[r]. Each slot holds exactly one group: slot owners[g] of prefix_cache holds group g's prefix, whose keys carry rotary encoding at positions 0 to 4095.
All inputs are finite; a program needn't handle non-finite values.
Results may differ from a plain program's by a relative error of at most 0.025.
Values may be sent and summed in bfloat16 or wider, within the bound.
A program may use at most 128 MiB of HBM per device.

v0:
```python
import math

import jax
import jax.numpy as jnp
from jax import lax
from jax.sharding import PartitionSpec as P

HD = 96
SUF = 512


rope_base = 100000.0
norm_eps = 1e-05
far_below = -1e30


def from_partner(block, axis, bit):
    count = lax.axis_size(axis)
    route = []
    for low in range(count):
        high = low | 1 << bit
        if high != low and high < count:
            route += [(low, high), (high, low)]
    return lax.ppermute(block, axis, route)


def rms_scale(row_values, norm_gain):
    numbers = row_values.astype(jnp.float32)
    mean_square = jnp.mean(numbers * numbers, axis=-1, keepdims=True)
    return numbers * lax.rsqrt(mean_square + norm_eps) * norm_gain.astype(jnp.float32)


def rotate(numbers, positions):
    half_width = numbers.shape[-1] // 2
    frequency = rope_base ** (
        -(jnp.arange(half_width).astype(jnp.float32) * 2.0 / numbers.shape[-1])
    )
    angles = positions[:, None] * frequency[None, :]
    cosine = jnp.cos(angles)[:, None, :]
    sine_part = jnp.sin(angles)[:, None, :]
    lower_half = numbers[..., :half_width]
    upper_half = numbers[..., half_width:]
    return jnp.concatenate(
        [
            lower_half * cosine - upper_half * sine_part,
            upper_half * cosine + lower_half * sine_part,
        ],
        axis=-1,
    )


def prefix_part(query_block, key_rows, value_rows, score_scale):
    scores = (
        jnp.einsum("hid,jd->hij", query_block, key_rows, preferred_element_type=jnp.float32)
        * score_scale
    )
    row_top = jnp.max(scores, axis=-1)
    weights = jnp.exp(scores - row_top[..., None])
    row_total = jnp.sum(weights, axis=-1)
    summed = jnp.einsum(
        "hij,jd->hid", weights.astype(jnp.bfloat16), value_rows, preferred_element_type=jnp.float32
    )
    return (row_top, row_total, summed)


def local(
    tokens,
    attention_gain,
    feed_gain,
    w_query,
    w_key,
    w_value,
    w_out,
    w_gate,
    w_up,
    w_down,
    prefix_cache,
    lengths,
    member,
    owners,
):
    w_query, w_key, w_value, w_gate, w_up = (
        lax.all_gather(w_query, "req", axis=0, tiled=True),
        lax.all_gather(w_key, "req", axis=0, tiled=True),
        lax.all_gather(w_value, "req", axis=0, tiled=True),
        lax.all_gather(w_gate, "req", axis=0, tiled=True),
        lax.all_gather(w_up, "req", axis=0, tiled=True),
    )
    w_out, w_down = (
        lax.all_gather(w_out, "req", axis=1, tiled=True),
        lax.all_gather(w_down, "req", axis=1, tiled=True),
    )
    model_devices = lax.axis_size("mdl")
    model_place = lax.axis_index("mdl")
    group_place = lax.axis_index("req")
    local_rows = tokens.shape[0]
    group_rows = local_rows * model_devices
    local_requests = group_rows // SUF
    query_width = w_query.shape[1]
    heads_here = query_width // HD
    pair_width = w_key.shape[1]
    halves = HD // pair_width
    prefix_length = prefix_cache.shape[2]
    score_scale = 1.0 / math.sqrt(HD)
    stacked_weights = jnp.concatenate([w_query, w_key, w_value], axis=1)
    normed = rms_scale(lax.all_gather(tokens, "mdl", axis=0, tiled=True), attention_gain).astype(
        jnp.bfloat16
    )
    projected = jnp.dot(normed, stacked_weights, preferred_element_type=jnp.float32)
    projected_pair = jnp.stack(
        [
            projected[:, query_width : query_width + pair_width],
            projected[:, query_width + pair_width :],
        ],
        axis=0,
    )
    own_prefix = prefix_cache[:, 0]
    low_half = model_place % 2 == 0
    partner = from_partner(projected_pair.astype(jnp.bfloat16), "mdl", 0).astype(
        projected_pair.dtype
    )
    full_pair = jnp.where(
        low_half,
        jnp.concatenate([projected_pair, partner], axis=2),
        jnp.concatenate([partner, projected_pair], axis=2),
    )
    prefix_partner = from_partner(own_prefix, "mdl", 0)
    prefix_full = jnp.where(
        low_half,
        jnp.concatenate([own_prefix, prefix_partner], axis=2),
        jnp.concatenate([prefix_partner, own_prefix], axis=2),
    )
    offsets = jnp.arange(group_rows, dtype=jnp.int32) % SUF
    positions = (offsets + prefix_length).astype(jnp.float32)
    queries = rotate(
        projected[:, :query_width].reshape(group_rows, heads_here, HD), positions
    ).astype(jnp.bfloat16)
    keys_rotated = rotate(full_pair[0].reshape(group_rows, 1, HD), positions).reshape(
        group_rows, HD
    )
    key_rows = keys_rotated.astype(jnp.bfloat16)
    value_rows = full_pair[1].astype(jnp.bfloat16)
    local_lengths = lax.dynamic_slice_in_dim(lengths, group_place * local_requests, local_requests)
    valid = jnp.arange(SUF, dtype=jnp.int32)[None, :] < local_lengths[:, None]
    valid_rows = valid.reshape(group_rows)
    own_start = model_place % halves * pair_width
    key_own = lax.dynamic_slice_in_dim(keys_rotated, own_start, pair_width, 1)
    cache_rows = jnp.stack([key_own, projected_pair[1]], axis=0) * valid_rows[None, :, None].astype(
        jnp.float32
    )
    suffix_cache = cache_rows.astype(jnp.bfloat16)
    query_blocks = queries.reshape(local_requests, SUF, heads_here, HD).transpose(0, 2, 1, 3)
    group_numbers = jnp.arange(owners.shape[0], dtype=jnp.int32)
    every_prefix = lax.all_gather(prefix_full[:, None], "req", axis=1, tiled=True)
    local_members = lax.dynamic_slice_in_dim(member, group_place * local_requests, local_requests)
    slot_ids = jnp.sum(
        jnp.where(local_members[:, None] == group_numbers[None, :], owners[None, :], 0), axis=1
    )

    def attend(request):
        slot_index = slot_ids[request]
        prefix_keys = lax.dynamic_index_in_dim(every_prefix[0], slot_index, 0, keepdims=False)
        prefix_values = lax.dynamic_index_in_dim(every_prefix[1], slot_index, 0, keepdims=False)
        return prefix_part(query_blocks[request], prefix_keys, prefix_values, score_scale)

    prefix_top, prefix_total, prefix_sum = lax.map(
        attend, jnp.arange(local_requests, dtype=jnp.int32)
    )
    key_blocks = key_rows.reshape(local_requests, SUF, HD)
    value_blocks = value_rows.reshape(local_requests, SUF, HD)
    scores = (
        jnp.einsum("rhid,rjd->rhij", query_blocks, key_blocks, preferred_element_type=jnp.float32)
        * score_scale
    )
    causal = jnp.arange(SUF)[:, None] >= jnp.arange(SUF)[None, :]
    allowed = (causal[None, :, :] & valid[:, None, :])[:, None]
    masked = jnp.where(allowed, scores, far_below)
    row_top = jnp.maximum(prefix_top, jnp.max(masked, axis=-1))
    carried_share = jnp.exp(prefix_top - row_top)
    weights = jnp.where(allowed, jnp.exp(masked - row_top[..., None]), 0.0)
    row_total = carried_share * prefix_total + jnp.sum(weights, axis=-1)
    summed = carried_share[..., None] * prefix_sum + jnp.einsum(
        "rhij,rjd->rhid",
        weights.astype(jnp.bfloat16),
        value_blocks,
        preferred_element_type=jnp.float32,
    )
    head_output = (summed / row_total[..., None]).astype(jnp.bfloat16)
    attended = head_output.transpose(0, 2, 1, 3).reshape(group_rows, query_width)
    attention_own = lax.psum_scatter(
        jnp.dot(attended, w_out, preferred_element_type=jnp.float32).astype(jnp.bfloat16),
        "mdl",
        scatter_dimension=0,
        tiled=True,
    ).astype(jnp.float32)
    residual = (tokens.astype(jnp.float32) + attention_own).astype(jnp.bfloat16)
    normed_mid = rms_scale(lax.all_gather(residual, "mdl", axis=0, tiled=True), feed_gain).astype(
        jnp.bfloat16
    )
    gate_value = jnp.dot(normed_mid, w_gate, preferred_element_type=jnp.float32)
    up_value = jnp.dot(normed_mid, w_up, preferred_element_type=jnp.float32)
    activation = (jax.nn.silu(gate_value) * up_value).astype(jnp.bfloat16)
    feed_own = lax.psum_scatter(
        jnp.dot(activation, w_down, preferred_element_type=jnp.float32).astype(jnp.bfloat16),
        "mdl",
        scatter_dimension=0,
        tiled=True,
    ).astype(jnp.float32)
    own_valid = lax.dynamic_slice_in_dim(valid_rows, model_place * local_rows, local_rows, 0)
    hidden = (
        (residual.astype(jnp.float32) + feed_own) * own_valid[:, None].astype(jnp.float32)
    ).astype(jnp.bfloat16)
    return (hidden, suffix_cache)


def solution(mesh):
    placed = (
        P(("req", "mdl"), None),
        P(),
        P(),
        P("req", "mdl"),
        P("req", "mdl"),
        P("req", "mdl"),
        P("mdl", "req"),
        P("req", "mdl"),
        P("req", "mdl"),
        P("mdl", "req"),
        P(None, "req", None, "mdl"),
        P(),
        P(),
        P(),
    )
    return jax.shard_map(
        local,
        mesh=mesh,
        in_specs=placed,
        out_specs=(P(("req", "mdl"), None), P(None, "req", "mdl")),
        check_vma=False,
    )
```

profile of v0, /device:TPU:1, one launch (start us, length us, event | category | flops | bytes accessed | tf_op | source)
XLA Modules:
  0.0 609.3 jit_solution(12306583454633041432)
XLA Ops:
  8.0 1.5 collective-permute-start
  9.5 2.1 collective-permute-done
  11.6 3.0 maximum_select_fusion
  14.7 28.8 %all-gather.1 = bf16[8,192,48]{1,2,0:T(8,128)(2,1)S(1)} all-gather(bf16[1,192,48]{1,2,0:T(8,128)(2,1)S(1)} %bitcast.110), channel_id=1, replica_groups=mesh['req'=8,'mdl'=16] {'req'}, dimensions={0}, use_global_device_ids=true | all-gather | bytes 165888 | tf_op jit(solution)/shard_map/all_gather | solution.py:85
  43.7 28.4 %all-gather = bf16[8,192,48]{1,2,0:T(8,128)(2,1)S(1)} all-gather(bf16[1,192,48]{1,2,0:T(8,128)(2,1)S(1)} %bitcast.111), channel_id=1, replica_groups=mesh['req'=8,'mdl'=16] {'req'}, dimensions={0}, use_global_device_ids=true | all-gather | bytes 165888 | tf_op jit(solution)/shard_map/all_gather | solution.py:84
  73.7 30.5 %all_gather.31 = bf16[1536,96]{1,0:T(8,128)(2,1)S(1)} all-gather(bf16[192,96]{1,0:T(8,128)(2,1)S(1)} %copy-done.9), channel_id=1, replica_groups=mesh['req'=8,'mdl'=16] {'req'}, dimensions={0}, use_global_device_ids=true | all-gather | bytes 331776 | tf_op jit(solution)/shard_map/all_gather | solution.py:83
  104.2 33.1 %all_gather.35 = bf16[96,1536]{0,1:T(8,128)(2,1)} all-gather(bf16[96,192]{0,1:T(8,128)(2,1)S(1)} %copy.93), channel_id=1, replica_groups=mesh['req'=8,'mdl'=16] {'req'}, dimensions={1}, use_global_device_ids=true | all-gather | bytes 331776 | tf_op jit(solution)/shard_map/all_gather | solution.py:90
  137.9 4.2 fusion.20
  142.5 2.7 fusion.26
  145.4 23.8 %collective-permute-start.1 = (bf16[2,2048,48]{1,2,0:T(8,128)(2,1)S(1)}, bf16[2,2048,48]{1,2,0:T(8,128)(2,1)S(1)}, u32[]{:S(2)}, u32[]{:S(2)}) collective-permute-start(bf16[2,2048,48]{1,2,0:T(8,128)(2,1)S(1)} %fusion.57), channel_id=1, source_target_pairs={{0,1},{1,0},{2,3},{3,2},{4,5},{5,4},{6,7},{7,6},{8,9},{9,8},{10,11... | collective-permute-start | bytes 1179656 | tf_op jit(solution)/shard_map/ppermute | solution.py:24
  169.2 1.3 collective-permute-done.1
  170.8 2.7 fusion.77
  174.6 1.7 concatenate.66
  180.3 1.6 copy.87
  183.3 1.3 pad_maximum_fusion.3
  184.6 3.6 fusion.30
  188.2 31.1 %all-gather.8.cloned.1.call-done = bf16[2,8,4096,96]{2,3,0,1:T(8,128)(2,1)} async-done(((bf16[2,1,4096,96]{2,3,0,1:T(8,128)(2,1)}), bf16[2,8,4096,96]{2,3,0,1:T(8,128)(2,1)}) %all-gather.8.cloned.1.call-update) | async-done | bytes 12582928 | tf_op jit(solution)/shard_map/all_gather | solution.py:154
  219.3 19.8 %copy.85 = bf16[2,8,4096,96]{3,2,1,0:T(8,128)(2,1)} copy(bf16[2,8,4096,96]{2,3,0,1:T(8,128)(2,1)} %all-gather.8.cloned.1.call-done) | data formatting | bytes 25165824 | tf_op jit(solution)/shard_map/while | solution.py:166
  239.1 67.7 %while.14 = (s32[]{:T(128)}, f32[4,1,512]{2,1,0:T(1,128)S(1)}, f32[4,1,512]{2,1,0:T(1,128)S(1)}, f32[4,1,512,96]{2,3,1,0:T(8,128)}, s32[4]{0:T(128)S(1)}, /*inde...) while((s32[]{:T(128)}, f32[4,1,512]{2,1,0:T(1,128)S(1)}, ...), condition=%wide.region_5.6_spmd, body=%wide.region_2.5_spmd.sunk | while | flops 822082560 | bytes 52773596 | solution.py:166
  244.2 6.5 %fusion.112 = (bf16[1,8,4096,96]{3,2,1,0:T(8,128)(2,1)S(1)}, bf16[1,8,4096,96]{3,2,1,0:T(8,128)(2,1)S(1)}) fusion(bf16[2,8,4096,96]{3,2,1,0:T(8,128)(2,1)} %get-tuple-element.202), kind=kLoop, calls=%fused_computation.127.clone.1 | loop fusion | bytes 25165824 | tf_op jit(solution)/shard_map/while/body/eval_jaxpr/slice | solution.py:163
  250.7 1.3 multiply_reduce_fusion.2
  252.0 2.5 fusion.114
  254.6 1.5 fusion.113
  261.1 6.5 %fusion.112 = (bf16[1,8,4096,96]{3,2,1,0:T(8,128)(2,1)S(1)}, bf16[1,8,4096,96]{3,2,1,0:T(8,128)(2,1)S(1)}) fusion(bf16[2,8,4096,96]{3,2,1,0:T(8,128)(2,1)} %get-tuple-element.202), kind=kLoop, calls=%fused_computation.127.clone.1 | loop fusion | bytes 25165824 | tf_op jit(solution)/shard_map/while/body/eval_jaxpr/slice | solution.py:163
  267.6 1.3 multiply_reduce_fusion.2
  269.0 2.5 fusion.114
  271.5 1.5 fusion.113
  278.1 6.5 %fusion.112 = (bf16[1,8,4096,96]{3,2,1,0:T(8,128)(2,1)S(1)}, bf16[1,8,4096,96]{3,2,1,0:T(8,128)(2,1)S(1)}) fusion(bf16[2,8,4096,96]{3,2,1,0:T(8,128)(2,1)} %get-tuple-element.202), kind=kLoop, calls=%fused_computation.127.clone.1 | loop fusion | bytes 25165824 | tf_op jit(solution)/shard_map/while/body/eval_jaxpr/slice | solution.py:163
  284.6 1.3 multiply_reduce_fusion.2
  285.9 2.5 fusion.114
  288.4 1.5 fusion.113
  295.0 6.5 %fusion.112 = (bf16[1,8,4096,96]{3,2,1,0:T(8,128)(2,1)S(1)}, bf16[1,8,4096,96]{3,2,1,0:T(8,128)(2,1)S(1)}) fusion(bf16[2,8,4096,96]{3,2,1,0:T(8,128)(2,1)} %get-tuple-element.202), kind=kLoop, calls=%fused_computation.127.clone.1 | loop fusion | bytes 25165824 | tf_op jit(solution)/shard_map/while/body/eval_jaxpr/slice | solution.py:163
  301.5 1.3 multiply_reduce_fusion.2
  302.9 2.5 fusion.114
  305.4 1.5 fusion.113
  306.9 3.2 fusion.32
  310.3 2.9 fusion.53
  313.6 4.5 convolution_convert_fusion.1
  318.5 75.4 %reduce-scatter.3.cloned.1.call-done = bf16[128,1536]{1,0:T(8,128)(2,1)} async-done(((bf16[2048,1536]{1,0:T(8,128)(2,1)}), bf16[128,1536]{1,0:T(8,128)(2,1)}) %reduce-scatter.3.cloned.1.call-update) | async-done | bytes 393232 | tf_op jit(solution)/shard_map/reduce_scatter | solution.py:190
  393.9 1.8 add_convert_fusion
  395.8 32.8 %all_gather.37 = bf16[1536,256]{1,0:T(8,128)(2,1)S(1)} all-gather(bf16[192,256]{1,0:T(8,128)(2,1)S(1)} %copy-done.7), channel_id=1, replica_groups=mesh['req'=8,'mdl'=16] {'req'}, dimensions={0}, use_global_device_ids=true | all-gather | bytes 884736 | tf_op jit(solution)/shard_map/all_gather | solution.py:86
  428.6 33.6 %all_gather.38 = bf16[1536,256]{1,0:T(8,128)(2,1)S(1)} all-gather(bf16[192,256]{1,0:T(8,128)(2,1)S(1)} %copy-done.8), channel_id=1, replica_groups=mesh['req'=8,'mdl'=16] {'req'}, dimensions={0}, use_global_device_ids=true | all-gather | bytes 884736 | tf_op jit(solution)/shard_map/all_gather | solution.py:87
  462.1 29.8 %all_gather.39 = bf16[256,1536]{0,1:T(8,128)(2,1)S(1)} all-gather(bf16[256,192]{0,1:T(8,128)(2,1)} %param.25), channel_id=1, replica_groups=mesh['req'=8,'mdl'=16] {'req'}, dimensions={1}, use_global_device_ids=true | all-gather | bytes 884736 | tf_op jit(solution)/shard_map/all_gather | solution.py:91
  492.0 4.2 fusion.23
  496.6 3.5 fusion.39
  500.1 10.5 %convolution_convert_fusion = bf16[2048,1536]{1,0:T(8,128)(2,1)} fusion(bf16[256,1536]{0,1:T(8,128)(2,1)S(1)} %all_gather.39, bf16[1536,256]{1,0:T(8,128)(2,1)S(1)} %all_gather.38, f32[2048,256]{1,0:T(8,128)} %fusion.39, bf16[2048,1536]{1,0:T(8,128)(2,1)} %all-gather.10.cloned.1.call-done, f32[1536]{0:T(1024)S(1)} %convert_element_type.161, ...), kind=kOutput, calls=%fused_computation.29 | convolution fusion | flops 3240099840 | bytes 16267264 | tf_op jit(solution)/shard_map/dot_general | solution.py:204
  512.2 88.8 %reduce-scatter.5.cloned.1.call-done = bf16[128,1536]{1,0:T(8,128)(2,1)} async-done(((bf16[2048,1536]{1,0:T(8,128)(2,1)}), bf16[128,1536]{1,0:T(8,128)(2,1)}) %reduce-scatter.5.cloned.1.call-update) | async-done | bytes 393232 | tf_op jit(solution)/shard_map/reduce_scatter | solution.py:203
  600.9 1.9 multiply_convert_fusion
  (107 shorter events, 18.0 us)
Async XLA Ops:
  7.2 7.5 %copy-start.11 = (bf16[192,48]{0,1:T(8,128)(2,1)S(1)}, bf16[192,48]{0,1:T(8,128)(2,1)}, u32[]{:S(2)}) copy-start(bf16[192,48]{0,1:T(8,128)(2,1)} %param.21) | copy-start | bytes 55300
  7.2 36.5 %copy-start.12 = (bf16[192,48]{0,1:T(8,128)(2,1)S(1)}, bf16[192,48]{0,1:T(8,128)(2,1)}, u32[]{:S(2)}) copy-start(bf16[192,48]{0,1:T(8,128)(2,1)} %param.20) | copy-start | bytes 55300
  7.2 65.2 %copy-start.15 = (bf16[1536]{0:T(1024)(128)(2,1)S(1)}, bf16[1536]{0:T(1024)(128)(2,1)}, u32[]{:S(2)}) copy-start(bf16[1536]{0:T(1024)(128)(2,1)} %param.17) | copy-start | bytes 9220
  7.2 65.2 %copy-start.17 = (s32[32]{0:T(128)S(1)}, s32[32]{0:T(128)}, u32[]{:S(2)}) copy-start(s32[32]{0:T(128)} %param.28) | copy-start | bytes 388
  7.2 65.3 %copy-start.18 = (s32[32]{0:T(128)S(1)}, s32[32]{0:T(128)}, u32[]{:S(2)}) copy-start(s32[32]{0:T(128)} %param.27) | copy-start | bytes 388
  7.2 65.3 %copy-start.10 = (bf16[96,192]{1,0:T(8,128)(2,1)S(1)}, bf16[96,192]{1,0:T(8,128)(2,1)}, u32[]{:S(2)}) copy-start(bf16[96,192]{1,0:T(8,128)(2,1)} %param.22) | copy-start | bytes 110596
  7.2 65.5 %copy-start.19 = (s32[8]{0:T(128)S(1)}, s32[8]{0:T(128)}, u32[]{:S(2)}) copy-start(s32[8]{0:T(128)} %param.29) | copy-start | bytes 100
  7.2 66.4 %copy-start.9 = (bf16[192,96]{1,0:T(8,128)(2,1)S(1)}, bf16[192,96]{1,0:T(8,128)(2,1)}, u32[]{:S(2)}) copy-start(bf16[192,96]{1,0:T(8,128)(2,1)} %param.19) | copy-start | bytes 110596
  7.2 130.7 %all-gather.6.cloned.1.call-start = ((), (), s32[]{:S(2)}) async-start(), calls=%async_computation.2 | async-start | bytes 6684672 | tf_op jit(solution)/shard_map/all_gather | solution.py:106
  8.0 211.3 %all-gather.8.cloned.1.call-start = ((), (), s32[]{:S(2)}) async-start(), calls=%async_computation.3 | async-start | bytes 14155776 | tf_op jit(solution)/shard_map/all_gather | solution.py:154
  8.0 3.6 collective-permute-start
  14.6 379.3 %reduce-scatter.3.cloned.1.call-start = ((), (), s32[]{:S(2)}) async-start(), calls=%async_computation.4 | async-start | bytes 6684672 | tf_op jit(solution)/shard_map/reduce_scatter | solution.py:190
  137.9 4.6 copy-start
  145.4 25.1 %collective-permute-start.1 = (bf16[2,2048,48]{1,2,0:T(8,128)(2,1)S(1)}, bf16[2,2048,48]{1,2,0:T(8,128)(2,1)S(1)}, u32[]{:S(2)}, u32[]{:S(2)}) collective-permute-start(bf16[2,2048,48]{1,2,0:T(8,128)(2,1)S(1)} %fusion.57), channel_id=1, source_target_pairs={{0,1},{1,0},{2,3},{3,2},{4,5},{5,4},{6,7},{7,6},{8,9},{9,8},{10,11... | collective-permute-start | bytes 1179656 | tf_op jit(solution)/shard_map/ppermute | solution.py:24
  178.2 6.4 %copy-start.6 = (pred[512,512]{0,1:T(8,128)(4,1)S(1)}, pred[512,512]{0,1:T(8,128)(4,1)}, u32[]{:S(2)}) copy-start(pred[512,512]{0,1:T(8,128)(4,1)} %iota_compare_fusion) | copy-start | bytes 786436
  188.2 50.9 %copy-start.14 = (f32[4,1,512]{2,1,0:T(1,128)S(1)}, f32[4,1,512]{2,1,0:T(1,128)}, u32[]{:S(2)}) copy-start(f32[4,1,512]{2,1,0:T(1,128)} %custom-call.1) | copy-start | bytes 24580
  306.9 3.5 copy-start.2
  310.3 3.3 copy-start.4
  318.1 75.7 %copy-start.5 = (bf16[128,1536]{1,0:T(8,128)(2,1)S(1)}, bf16[128,1536]{1,0:T(8,128)(2,1)}, u32[]{:S(2)}) copy-start(bf16[128,1536]{1,0:T(8,128)(2,1)} %param.16) | copy-start | bytes 1179652
  318.1 77.6 %copy-start.16 = (bf16[1536]{0:T(1024)(128)(2,1)S(1)}, bf16[1536]{0:T(1024)(128)(2,1)}, u32[]{:S(2)}) copy-start(bf16[1536]{0:T(1024)(128)(2,1)} %param.18) | copy-start | bytes 9220
  318.1 77.6 %copy-start.7 = (bf16[192,256]{1,0:T(8,128)(2,1)S(1)}, bf16[192,256]{1,0:T(8,128)(2,1)}, u32[]{:S(2)}) copy-start(bf16[192,256]{1,0:T(8,128)(2,1)} %param.23) | copy-start | bytes 294916
  318.2 110.4 %copy-start.8 = (bf16[192,256]{1,0:T(8,128)(2,1)S(1)}, bf16[192,256]{1,0:T(8,128)(2,1)}, u32[]{:S(2)}) copy-start(bf16[192,256]{1,0:T(8,128)(2,1)} %param.24) | copy-start | bytes 294916
  318.2 173.8 %all-gather.10.cloned.1.call-start = ((), (), s32[]{:S(2)}) async-start(), calls=%async_computation.5 | async-start | bytes 6684672 | tf_op jit(solution)/shard_map/all_gather | solution.py:197
  395.7 205.2 %reduce-scatter.5.cloned.1.call-start = ((), (), s32[]{:S(2)}) async-start(), calls=%async_computation.6 | async-start | bytes 6684672 | tf_op jit(solution)/shard_map/reduce_scatter | solution.py:203
  492.0 4.6 copy-start.1
  510.6 0.6 copy-start.13
  510.6 90.4 %copy-start.3 = (bf16[128,1536]{1,0:T(8,128)(2,1)S(1)}, bf16[128,1536]{1,0:T(8,128)(2,1)}, u32[]{:S(2)}) copy-start(bf16[128,1536]{1,0:T(8,128)(2,1)} %add_convert_fusion) | copy-start | bytes 1179652
Sparse Core Ops, SparseCore 0:
  9.8 49.1 all-gather.5
  61.2 158.0 all-gather.7
  318.3 75.5 reduce-scatter.2
  396.0 66.6 all-gather.9
  510.7 90.1 reduce-scatter.4
where the time goes:
time: 612 us; the launch traced here: 609 us
  blocking collectives  217 us (35%)
  waiting for transfers between devices  199 us (33%)
  local copies, waits for them, and re-layouts  63 us (10%)
  matrix products  43.1 us (7%)
  other arithmetic  31.2 us (5%)
  starting transfers between devices  25.7 us (4%)
  loops' own time  15.6 us (3%)
  between operations  14.2 us (2%)
    reduce_scatter x1, waiting for transfers between devices, local(): lax.psum_scatter(jnp.dot(activation, w_down, preferred_element_type=jnp.f...  88.8 us
    reduce_scatter x1, waiting for transfers between devices, local(): lax.psum_scatter(jnp.dot(attended, w_out, preferred_element_type=jnp.floa...  75.4 us
    all_gather x1, blocking collectives, local(): lax.all_gather(w_up, 'req', axis=0, tiled=True)  33.6 us
    all_gather x1, blocking collectives, local(): lax.all_gather(w_out, 'req', axis=1, tiled=True)  33.1 us
    all_gather x1, blocking collectives, local(): lax.all_gather(w_gate, 'req', axis=0, tiled=True)  32.8 us
    all_gather x1, waiting for transfers between devices, local(): lax.all_gather(prefix_full[:, None], 'req', axis=1, tiled=True)  31.1 us
    all_gather x1, blocking collectives, local(): lax.all_gather(w_query, 'req', axis=0, tiled=True)  30.5 us
    all_gather x1, blocking collectives, local(): lax.all_gather(w_down, 'req', axis=1, tiled=True)  29.8 us
  transfers between devices with their start and end apart: 7, of which 5 were waited for; matrix products, arithmetic and copies ran while one was open for 5% of the time, Pallas kernels for 0%

commit v1 on v0

v1 whole, which is shorter than its diff:
```python
import functools
import math

import jax
import jax.numpy as jnp
from jax import lax
from jax.experimental import pallas as pl
from jax.experimental.pallas import tpu as pltpu
from jax.sharding import PartitionSpec as P

HD = 96
HALF = 48
SUF = 512
rope_base = 100000.0
norm_eps = 1e-05
MESH = pl.DeviceIdType.MESH
LOG2E = 1.4426950408889634


def places():
    req = lax.axis_index("req")
    mdl = lax.axis_index("mdl")
    return req, mdl


class Spread:
    def __init__(self, own, block, piece, ring, pair, dev, partner, send, recv):
        self.own, self.block, self.piece = own, block, piece
        self.u, self.v, self.dev, self.partner = ring, pair, dev, partner
        self.send, self.recv, self.made = send, recv, []

    def copy(self, index, src, dst, device):
        made = pltpu.make_async_remote_copy(
            src_ref=src,
            dst_ref=dst,
            send_sem=self.send.at[index],
            recv_sem=self.recv.at[index],
            device_id=device,
            device_id_type=MESH,
        )
        made.start()
        self.made.append(made)
        return made

    def at(self, du, flip):
        return self.block(lax.rem(self.u + du, 4), 1 - self.v if flip else self.v)

    def ring_dev(self, du):
        return self.dev(lax.rem(self.u + du, 4), self.v)

    def start(self):
        here = self.at(0, False)
        self.pair_copy = self.copy(0, self.own, here, self.dev(self.u, 1 - self.v))
        self.up = self.copy(1, self.own, here, self.ring_dev(1))
        self.down = self.copy(2, self.own, here, self.ring_dev(3))
        self.own_p = self.copy(3, self.own, here, self.partner)

    def pair_arrived(self):
        self.pair_copy.wait_recv()
        other = self.at(0, True)
        self.up2 = self.copy(4, other, other, self.ring_dev(1))
        self.down2 = self.copy(5, other, other, self.ring_dev(3))
        self.copy(6, other, other, self.partner)

    def ring_arrived(self, flip):
        base = 7 + 4 * flip
        (self.up2 if flip else self.up).wait_recv()
        low = self.at(3, flip)
        a = self.copy(base, self.piece(low, 0), self.piece(low, 0), self.ring_dev(1))
        (self.down2 if flip else self.down).wait_recv()
        high = self.at(1, flip)
        b = self.copy(base + 1, self.piece(high, 1), self.piece(high, 1), self.ring_dev(3))
        self.copy(base + 2, low, low, self.partner)
        self.copy(base + 3, high, high, self.partner)
        if flip:
            self.far2 = (a, b)
        else:
            self.far = (a, b)

    def far_arrived(self, flip):
        base = 15 + 2 * flip
        for h, made in enumerate(self.far2 if flip else self.far):
            made.wait_recv()
            place = self.piece(self.at(2, flip), h)
            self.copy(base + h, place, place, self.partner)

    def finish(self):
        self.awaited = [
            self.pair_copy, self.up, self.down, self.up2, self.down2, *self.far, *self.far2
        ]
        for made in self.made:
            made.wait_send()
        for made in self.made:
            if all(made is not other for other in self.awaited):
                made.wait_recv()


SPREAD_SEMS = 19


def gather_kernel(kv_in, tok_in, kv_out, tok_out, kv_send, kv_recv, tok_send, tok_recv, local_sem):
    req, mdl = places()
    x, yh = req // 2, lax.rem(req, 2)
    z, yl, core = mdl // 4, lax.rem(mdl // 2, 2), lax.rem(mdl, 2)
    partner = {"req": req, "mdl": z * 4 + yl * 2 + 1 - core}
    rows = pl.ds(pl.multiple_of(core * HALF, HALF), HALF)

    def kv_dev(u, v):
        return {"req": u * 2 + v, "mdl": mdl}

    def tok_dev(u, v):
        return {"req": req, "mdl": u * 4 + v * 2 + core}

    barrier = pltpu.get_barrier_semaphore()
    peers = [
        partner,
        kv_dev(x, 1 - yh),
        kv_dev(lax.rem(x + 1, 4), yh),
        kv_dev(lax.rem(x + 3, 4), yh),
        tok_dev(z, 1 - yl),
        tok_dev(lax.rem(z + 1, 4), yl),
        tok_dev(lax.rem(z + 3, 4), yl),
    ]
    for peer in peers:
        pl.semaphore_signal(barrier, inc=1, device_id=peer, device_id_type=MESH)
    pl.semaphore_wait(barrier, len(peers))

    kv = Spread(
        kv_in,
        lambda u, v: kv_out.at[u * 2 + v, :, rows, :],
        lambda ref, h: ref.at[h],
        x, yh, kv_dev, partner, kv_send, kv_recv,
    )
    tok = Spread(
        tok_in,
        lambda u, v: tok_out.at[u * 4 + v * 2 + core],
        lambda ref, h: ref.at[pl.ds(64 * h, 64)],
        z, yl, tok_dev, partner, tok_send, tok_recv,
    )
    tok.start()
    kv.start()
    keep_kv = pltpu.make_async_copy(kv_in, kv.at(0, False), local_sem.at[0])
    keep_tok = pltpu.make_async_copy(tok_in, tok.at(0, False), local_sem.at[1])
    keep_kv.start()
    keep_tok.start()
    tok.pair_arrived()
    tok.ring_arrived(False)
    kv.ring_arrived(False)
    tok.ring_arrived(True)
    kv.pair_arrived()
    tok.far_arrived(False)
    tok.far_arrived(True)
    kv.far_arrived(False)
    kv.ring_arrived(True)
    kv.far_arrived(True)
    keep_kv.wait()
    keep_tok.wait()
    tok.finish()
    kv.finish()


def gather(kv_own, tokens):
    width = tokens.shape[1]
    return pl.pallas_call(
        gather_kernel,
        out_shape=(
            jax.ShapeDtypeStruct((8, 2, HD, kv_own.shape[2]), jnp.bfloat16),
            jax.ShapeDtypeStruct((16, tokens.shape[0], width), jnp.bfloat16),
        ),
        in_specs=[pl.BlockSpec(memory_space=pltpu.VMEM)] * 2,
        out_specs=[pl.BlockSpec(memory_space=pl.ANY)] * 2,
        scratch_shapes=[pltpu.SemaphoreType.DMA((SPREAD_SEMS,))] * 4
        + [pltpu.SemaphoreType.DMA((2,))],
        compiler_params=pltpu.CompilerParams(collective_id=0, has_side_effects=True),
        name="gather_kernel",
    )(kv_own, tokens)


def attend_kernel(
    slots, lens, tok_ref, gain_ref, w_ref, cos_ref, sin_ref, kv_ref, att_ref, cache_ref, kv_width
):
    request = pl.program_id(0)
    length = lens[request]
    core = lens[4]
    numbers = tok_ref[...].astype(jnp.float32)
    scale = lax.rsqrt(jnp.mean(numbers * numbers, axis=-1, keepdims=True) + norm_eps)
    normed = (numbers * scale * gain_ref[...].astype(jnp.float32)).astype(jnp.bfloat16)
    projected = lax.dot_general(
        w_ref[...], normed, (((1,), (1,)), ((), ())), preferred_element_type=jnp.float32
    )
    cosine, sine = cos_ref[...], sin_ref[...]

    def rotate(block):
        low, high = block[:HALF], block[HALF:]
        return jnp.concatenate(
            [low * cosine - high * sine, high * cosine + low * sine], axis=0
        )

    query = jnp.transpose(rotate(projected[:HD])).astype(jnp.bfloat16)
    keys_wide = rotate(projected[HD : 2 * HD])
    values_wide = projected[2 * HD :]
    keys = keys_wide.astype(jnp.bfloat16)
    values = values_wide.astype(jnp.bfloat16)
    live = (lax.broadcasted_iota(jnp.int32, (HALF, SUF), 1) < length).astype(jnp.float32)
    first = core == 0
    cache_ref[0] = (
        jnp.where(first, keys_wide[:HALF], keys_wide[HALF:]) * live
    ).astype(jnp.bfloat16)
    cache_ref[1] = (
        jnp.where(first, values_wide[:HALF], values_wide[HALF:]) * live
    ).astype(jnp.bfloat16)

    factor = LOG2E / math.sqrt(HD)
    top = total = summed = None
    chunk = 1024
    pieces = [
        (kv_ref[0, 0, :, j : j + chunk], kv_ref[0, 1, :, j : j + chunk], False)
        for j in range(0, kv_width, chunk)
    ] + [(keys, values, True)]
    for key_part, value_part, own in pieces:
        scores = jnp.dot(query, key_part, preferred_element_type=jnp.float32)
        if own:
            row = lax.broadcasted_iota(jnp.int32, scores.shape, 0)
            column = lax.broadcasted_iota(jnp.int32, scores.shape, 1)
            allowed = (column <= row) & (column < length)
            scores = jnp.where(allowed, scores, -1e30)
        part_top = jnp.max(scores, axis=-1, keepdims=True)
        new_top = part_top if top is None else jnp.maximum(top, part_top)
        weights = jnp.exp2((scores - new_top) * factor)
        if own:
            weights = jnp.where(allowed, weights, 0.0)
        part_total = jnp.sum(weights, axis=-1, keepdims=True)
        part_sum = lax.dot_general(
            weights.astype(jnp.bfloat16),
            value_part,
            (((1,), (1,)), ((), ())),
            preferred_element_type=jnp.float32,
        )
        if top is None:
            total, summed = part_total, part_sum
        else:
            carried = jnp.exp2((top - new_top) * factor)
            total = total * carried + part_total
            summed = summed * carried + part_sum
        top = new_top
    att_ref[0] = jnp.transpose(summed / total).astype(jnp.bfloat16)


def attend(slots, lens, tokens, gain, weights, cosine, sine, kv_all):
    requests = 4
    width = tokens.shape[1]
    kv_width = kv_all.shape[3]
    whole = lambda r, *_: (0, 0)
    spec = pltpu.PrefetchScalarGridSpec(
        num_scalar_prefetch=2,
        grid=(requests,),
        in_specs=[
            pl.BlockSpec((SUF, width), lambda r, *_: (r, 0)),
            pl.BlockSpec((1, width), whole),
            pl.BlockSpec(weights.shape, whole),
            pl.BlockSpec((HALF, SUF), whole),
            pl.BlockSpec((HALF, SUF), whole),
            pl.BlockSpec((1, 2, HD, kv_width), lambda r, slots, lens: (slots[r], 0, 0, 0)),
        ],
        out_specs=[
            pl.BlockSpec((1, HD, SUF), lambda r, *_: (r, 0, 0)),
            pl.BlockSpec((2, HALF, SUF), lambda r, *_: (0, 0, r)),
        ],
    )
    return pl.pallas_call(
        functools.partial(attend_kernel, kv_width=kv_width),
        grid_spec=spec,
        out_shape=(
            jax.ShapeDtypeStruct((requests, HD, SUF), jnp.bfloat16),
            jax.ShapeDtypeStruct((2, HALF, requests * SUF), jnp.bfloat16),
        ),
        compiler_params=pltpu.CompilerParams(
            dimension_semantics=("arbitrary",), vmem_limit_bytes=60 << 20
        ),
        cost_estimate=pl.CostEstimate(
            flops=6_000_000_000, bytes_accessed=20_000_000, transcendentals=10_000_000
        ),
        name="attend_kernel",
    )(slots, lens, tokens, gain, weights, cosine, sine, kv_all)


def feed_kernel(
    att_in, tok_in, gain_ref, wo_hbm, wm_hbm, out_ref,
    att, wo, wm, rows_all, part, from_pair, sums, relay, plain, joined, to_relay,
    a2a_send, a2a_recv, send, recv, w_sem,
):
    req, mdl = places()
    z, yl, core = mdl // 4, lax.rem(mdl // 2, 2), lax.rem(mdl, 2)

    def peer(du, flip=False):
        other = 1 - core if flip else core
        return {"req": req, "mdl": lax.rem(z + du, 4) * 4 + yl * 2 + other}

    barrier = pltpu.get_barrier_semaphore()
    for step in range(1, 16):
        pl.semaphore_signal(
            barrier,
            inc=1,
            device_id={"req": req, "mdl": lax.rem(mdl + step, 16)},
            device_id_type=MESH,
        )
    fetch = [pltpu.make_async_copy(wo_hbm, wo, w_sem.at[0])]
    for block in range(2):
        for kind in range(3):
            fetch.append(
                pltpu.make_async_copy(
                    wm_hbm.at[:, block, kind], wm.at[block, kind], w_sem.at[1 + 3 * block + kind]
                )
            )
    for made in fetch:
        made.start()
    pl.semaphore_wait(barrier, 15)

    def remote(src, dst, device, sends, recvs, index):
        made = pltpu.make_async_remote_copy(
            src_ref=src,
            dst_ref=dst,
            send_sem=sends.at[index],
            recv_sem=recvs.at[index],
            device_id=device,
            device_id_type=MESH,
        )
        made.start()
        return made

    exchange = []
    for step in range(1, 16):
        target = lax.rem(mdl + step, 16)
        columns = pl.ds(pl.multiple_of(lax.rem(target, 4) * 128, 128), 128)
        exchange.append(
            remote(
                att_in.at[target // 4, :, columns],
                att.at[mdl],
                {"req": req, "mdl": target},
                a2a_send,
                a2a_recv,
                step - 1,
            )
        )
    columns = pl.ds(pl.multiple_of(lax.rem(mdl, 4) * 128, 128), 128)
    att[mdl] = att_in[z, :, columns]
    for made in exchange:
        made.wait_recv()
    fetch[0].wait()
    width = tok_in.shape[1]
    attended = jnp.transpose(att[...].reshape(16 * HD, 128))
    own_rows = rows_all.at[z, core]
    for column in range(0, width, 512):
        here = slice(column, column + 512)
        attention = jnp.dot(attended, wo[:, here], preferred_element_type=jnp.float32)
        own_rows[:, here] = (tok_in[:, here].astype(jnp.float32) + attention).astype(jnp.bfloat16)

    made = []

    def go(src, dst, device, index):
        copy = remote(src, dst, device, send, recv, index)
        made.append(copy)
        return copy

    up = go(own_rows, own_rows, peer(1), 0)
    down = go(own_rows, own_rows, peer(3), 1)
    across = go(own_rows, own_rows, peer(0, True), 2)
    for copy in fetch[1:]:
        copy.wait()

    def feed(slot, du):
        there = rows_all.at[lax.rem(z + du, 4)]
        numbers = there[...].reshape(256, width).astype(jnp.float32)
        scale = lax.rsqrt(jnp.mean(numbers * numbers, axis=-1, keepdims=True) + norm_eps)
        normed = (numbers * scale * gain_ref[...].astype(jnp.float32)).astype(jnp.bfloat16)
        active = []
        for block in range(2):
            gate = jnp.dot(
                normed,
                wm[block, 0].reshape(width, 256),
                preferred_element_type=jnp.float32,
            )
            lift = jnp.dot(
                normed,
                wm[block, 1].reshape(width, 256),
                preferred_element_type=jnp.float32,
            )
            active.append((gate / (1.0 + jnp.exp(-gate)) * lift).astype(jnp.bfloat16))
        for column in range(0, width, 384):
            parts = [
                lax.dot_general(
                    active[block],
                    wm[block, 2].reshape(width, 256)[column : column + 384],
                    (((1,), (1,)), ((), ())),
                    preferred_element_type=jnp.float32,
                )
                for block in range(2)
            ]
            part[slot, :, :, column : column + 384] = (
                (parts[0] + parts[1]).astype(jnp.bfloat16).reshape(2, 128, 384)
            )
        return go(part.at[slot, 1 - core], from_pair.at[slot], peer(0, True), 3 + slot)

    def pair_sum(slot, copy):
        copy.wait_recv()
        sums[slot] = part[slot, core].astype(jnp.float32) + from_pair[slot].astype(jnp.float32)

    across.wait_recv()
    pair0 = feed(0, 0)
    up.wait_recv()
    low = rows_all.at[lax.rem(z + 3, 4), core]
    far_a = go(low.at[pl.ds(0, 64)], low.at[pl.ds(0, 64)], peer(1), 7)
    low_p = go(low, low, peer(0, True), 8)
    down.wait_recv()
    high = rows_all.at[lax.rem(z + 1, 4), core]
    far_b = go(high.at[pl.ds(64, 64)], high.at[pl.ds(64, 64)], peer(3), 9)
    high_p = go(high, high, peer(0, True), 10)
    low_p.wait_recv()
    pair3 = feed(3, 3)
    high_p.wait_recv()
    pair1 = feed(1, 1)
    far = rows_all.at[lax.rem(z + 2, 4), core]
    far_a.wait_recv()
    far_pa = go(far.at[pl.ds(0, 64)], far.at[pl.ds(0, 64)], peer(0, True), 11)
    far_b.wait_recv()
    far_pb = go(far.at[pl.ds(64, 64)], far.at[pl.ds(64, 64)], peer(0, True), 12)
    pair_sum(3, pair3)
    plain[0] = sums[3, 0:64].astype(jnp.bfloat16)
    plain_a = go(plain.at[0], plain.at[2], peer(3), 13)
    pair_sum(1, pair1)
    plain[1] = sums[1, 64:128].astype(jnp.bfloat16)
    plain_b = go(plain.at[1], plain.at[3], peer(1), 14)
    far_pa.wait_recv()
    far_pb.wait_recv()
    pair2 = feed(2, 2)
    pair_sum(2, pair2)
    to_relay[...] = sums[2].astype(jnp.bfloat16)
    relay_a = go(to_relay.at[pl.ds(0, 64)], relay.at[0], peer(1), 15)
    relay_b = go(to_relay.at[pl.ds(64, 64)], relay.at[1], peer(3), 16)
    pair_sum(0, pair0)
    relay_a.wait_recv()
    joined[0] = (sums[1, 0:64] + relay[0].astype(jnp.float32)).astype(jnp.bfloat16)
    joined_a = go(joined.at[0], joined.at[2], peer(1), 17)
    relay_b.wait_recv()
    joined[1] = (sums[3, 64:128] + relay[1].astype(jnp.float32)).astype(jnp.bfloat16)
    joined_b = go(joined.at[1], joined.at[3], peer(3), 18)
    plain_a.wait_recv()
    plain_b.wait_recv()
    joined_a.wait_recv()
    joined_b.wait_recv()
    for h in range(2):
        here = slice(64 * h, 64 * h + 64)
        feed_sum = (
            sums[0, here]
            + plain[2 + h].astype(jnp.float32)
            + joined[2 + h].astype(jnp.float32)
        )
        out_ref[here, :] = (own_rows[here, :].astype(jnp.float32) + feed_sum).astype(jnp.bfloat16)
    for copy in exchange:
        copy.wait_send()
    for copy in made:
        copy.wait_send()


def feed_forward(att, tokens, gain, w_out, w_mlp):
    rows, width = tokens.shape
    vmem = pl.BlockSpec(memory_space=pltpu.VMEM)
    anywhere = pl.BlockSpec(memory_space=pl.ANY)
    bf16, f32 = jnp.bfloat16, jnp.float32
    return pl.pallas_call(
        feed_kernel,
        out_shape=jax.ShapeDtypeStruct((rows, width), bf16),
        in_specs=[vmem, vmem, vmem, anywhere, anywhere],
        out_specs=vmem,
        scratch_shapes=[
            pltpu.VMEM((16, HD, 128), bf16),
            pltpu.VMEM((width, width), bf16),
            pltpu.VMEM((2, 3, 8, 192, 256), bf16),
            pltpu.VMEM((4, 2, rows, width), bf16),
            pltpu.VMEM((4, 2, rows, width), bf16),
            pltpu.VMEM((4, rows, width), bf16),
            pltpu.VMEM((4, rows, width), f32),
            pltpu.VMEM((2, 64, width), bf16),
            pltpu.VMEM((4, 64, width), bf16),
            pltpu.VMEM((4, 64, width), bf16),
            pltpu.VMEM((rows, width), bf16),
            pltpu.SemaphoreType.DMA((15,)),
            pltpu.SemaphoreType.DMA((15,)),
            pltpu.SemaphoreType.DMA((19,)),
            pltpu.SemaphoreType.DMA((19,)),
            pltpu.SemaphoreType.DMA((7,)),
        ],
        compiler_params=pltpu.CompilerParams(
            collective_id=1, has_side_effects=True, vmem_limit_bytes=60 << 20
        ),
        name="feed_kernel",
    )(att, tokens, gain, w_out, w_mlp)


def local(
    tokens,
    attention_gain,
    feed_gain,
    w_query,
    w_key,
    w_value,
    w_out,
    w_gate,
    w_up,
    w_down,
    prefix_cache,
    lengths,
    member,
    owners,
):
    req, mdl = places()
    core = mdl % 2
    low_half = core == 0
    prefix_length = prefix_cache.shape[2]
    kv_own = prefix_cache[:, 0].transpose(0, 2, 1)
    own_kv = jnp.stack([w_key, w_value], axis=0)
    swap = [(m, m ^ 1) for m in range(16)]
    other_kv = lax.ppermute(own_kv, "mdl", swap)
    even = jnp.where(low_half, own_kv, other_kv)
    odd = jnp.where(low_half, other_kv, own_kv)
    packed = jnp.concatenate([w_query, even[0], odd[0], even[1], odd[1]], axis=1)
    w_qkv = lax.all_gather(packed, "req", axis=0, tiled=True).T
    mlp_own = jnp.stack([w_gate, w_up, w_down.T], axis=0)
    groups = [
        [r * 16 + z * 4 + y * 2 + c for r in range(8) for y in range(2)]
        for z in range(4)
        for c in range(2)
    ]
    w_mlp = lax.all_gather(mlp_own, ("req", "mdl"), axis_index_groups=groups).reshape(
        8, 2, 3, 192, 256
    )
    w_out_rows = lax.all_gather(w_out, "req", axis=1, tiled=True)
    w_out_all = lax.all_gather(w_out_rows, "mdl", axis=0, tiled=True)

    kv_all, tok_all = gather(kv_own, tokens)

    half = HD // 2
    frequency = rope_base ** (-(jnp.arange(half).astype(jnp.float32) * 2.0 / HD))
    positions = (jnp.arange(SUF, dtype=jnp.int32) + prefix_length).astype(jnp.float32)
    angles = positions[:, None] * frequency[None, :]
    local_lengths = lax.dynamic_slice_in_dim(lengths, req * 4, 4)
    local_members = lax.dynamic_slice_in_dim(member, req * 4, 4)
    group_numbers = jnp.arange(owners.shape[0], dtype=jnp.int32)
    slots = jnp.sum(
        jnp.where(local_members[:, None] == group_numbers[None, :], owners[None, :], 0), axis=1
    )
    lens = jnp.concatenate([local_lengths, core[None].astype(jnp.int32)])
    att, cache = attend(
        slots,
        lens,
        tok_all.reshape(16 * tokens.shape[0], tokens.shape[1]),
        attention_gain[None, :],
        w_qkv,
        jnp.cos(angles).T,
        jnp.sin(angles).T,
        kv_all,
    )
    hidden = feed_forward(att, tokens, feed_gain[None, :], w_out_all, w_mlp)
    own_offset = (mdl % 4) * tokens.shape[0] + jnp.arange(tokens.shape[0], dtype=jnp.int32)
    own_length = lax.dynamic_index_in_dim(local_lengths, mdl // 4, keepdims=False)
    own_valid = own_offset < own_length
    hidden = (hidden.astype(jnp.float32) * own_valid[:, None].astype(jnp.float32)).astype(
        jnp.bfloat16
    )
    return (hidden, cache.transpose(0, 2, 1))


def solution(mesh):
    placed = (
        P(("req", "mdl"), None),
        P(),
        P(),
        P("req", "mdl"),
        P("req", "mdl"),
        P("req", "mdl"),
        P("mdl", "req"),
        P("req", "mdl"),
        P("req", "mdl"),
        P("mdl", "req"),
        P(None, "req", None, "mdl"),
        P(),
        P(),
        P(),
    )
    return jax.shard_map(
        local,
        mesh=mesh,
        in_specs=placed,
        out_specs=(P(("req", "mdl"), None), P(None, "req", "mdl")),
        check_vma=False,
    )
```

time: 612 us -> 270 us (0.44)
  waiting for transfers between devices: 199 us -> 0.07 us
  Pallas kernels: 0 us -> 167 us
  blocking collectives: 217 us -> 63.8 us
  local copies, waits for them, and re-layouts: 63 us -> 10.3 us
  matrix products: 43.1 us -> 0 us
  other arithmetic: 31.2 us -> 7.53 us
  starting transfers between devices: 25.7 us -> 6.51 us
  loops' own time: 15.6 us -> 0 us
    pallas_call x0 -> x3, Pallas kernels: none -> 167 us  [the longest x1 92.9 us: gather(): pl.pallas_call(gather_kernel, out_shape=(jax.ShapeDtypeStruct((8, 2, HD,...]
    reduce_scatter x2 -> x0, waiting for transfers between devices: 164 us -> none  [the longest x1 88.8 us: local(): lax.psum_scatter(jnp.dot(activation, w_down, preferred_element_type=jnp.f...]
    all_gather x7 -> x2, blocking collectives: 217 us -> 63.8 us  [the longest x1 33.9 us: local(): w_qkv = lax.all_gather(packed, 'req', axis=0, tiled=True).T]
    dot_general x14 -> x0, matrix products: 43.1 us -> none  [the longest x1 10.5 us: local(): jnp.dot(activation, w_down, preferred_element_type=jnp.float32)]
    all_gather x3 -> x2, waiting for transfers between devices: 31.1 us -> 0.03 us  [the longest x1 0.02 us: local(): lax.all_gather(mlp_own, ('req', 'mdl'), axis_index_groups=groups)]
    slice x5 -> x0, local copies, waits for them, and re-layouts: 26.7 us -> none  [the longest x4 25.9 us: attend(): every_prefix[1]]
    while x1 -> x0, local copies, waits for them, and re-layouts: 19.8 us -> none  [local(): lax.map(attend, jnp.arange(local_requests, dtype=jnp.int32))]
    ppermute x2 -> x1, starting transfers between devices: 25.2 us -> 6.43 us  [local(): other_kv = lax.ppermute(own_kv, 'mdl', swap)]
  transfers between devices with their start and end apart: 7 -> 3, of which waited for: 5 -> 0; matrix products, arithmetic and copies ran while one was open for 5% -> 5% of each run, Pallas kernels for 0% -> 42%
where the time goes in v1:
time: 270 us; the launch traced here: 269 us
  Pallas kernels  167 us (62%)
  blocking collectives  63.8 us (24%)
  between operations  14.1 us (5%)
  local copies, waits for them, and re-layouts  10.3 us (4%)
  other arithmetic  7.53 us (3%)
  starting transfers between devices  6.51 us (2%)
    pallas_call x1, Pallas kernels, gather(): pl.pallas_call(gather_kernel, out_shape=(jax.ShapeDtypeStruct((8, 2, HD,...  92.9 us
    pallas_call x1, Pallas kernels, feed_forward(): pl.pallas_call(feed_kernel, out_shape=jax.ShapeDtypeStruct((rows, width),...  53.2 us
    all_gather x1, blocking collectives, local(): w_qkv = lax.all_gather(packed, 'req', axis=0, tiled=True).T  33.9 us
    all_gather x1, blocking collectives, local(): w_out_rows = lax.all_gather(w_out, 'req', axis=1, tiled=True)  29.9 us
    pallas_call x1, Pallas kernels, attend(): pl.pallas_call(functools.partial(attend_kernel, kv_width=kv_width), grid_...  20.9 us
    ppermute x1, starting transfers between devices, local(): other_kv = lax.ppermute(own_kv, 'mdl', swap)  6.43 us
  transfers between devices with their start and end apart: 3, of which 0 were waited for; matrix products, arithmetic and copies ran while one was open for 5% of the time, Pallas kernels for 42%

profile of v1, /device:TPU:1, one launch (start us, length us, event | category | flops | bytes accessed | tf_op | source)
XLA Modules:
  0.0 269.4 jit_solution(11060943844763119330)
XLA Ops:
  7.2 0.0 copy-start
  7.2 0.0 all-gather.4.cloned.1.call-start
  7.2 0.9 copy.25
  8.1 29.9 %all_gather.16 = bf16[96,1536]{0,1:T(8,128)(2,1)S(1)} all-gather(bf16[96,192]{0,1:T(8,128)(2,1)S(1)} %copy.25), channel_id=1, replica_groups=mesh['req'=8,'mdl'=16] {'req'}, dimensions={1}, use_global_device_ids=true | all-gather | bytes 331776 | tf_op jit(solution)/shard_map/all_gather | solution.py:537
  38.0 0.9 copy.26
  38.9 0.0 all-gather.4.cloned.1.call-update
  38.9 0.0 all-gather.6.cloned.1.call-start
  39.0 1.8 pad_maximum_fusion
  40.7 0.0 all-gather.6.cloned.1.call-update
  40.7 0.8 copy.22
  41.6 0.9 copy.23
  42.5 6.4 %collective-permute-start = (bf16[2,192,48]{2,1,0:T(8,128)(2,1)S(1)}, bf16[2,192,48]{2,1,0:T(8,128)(2,1)S(1)}, u32[]{:S(2)}, u32[]{:S(2)}) collective-permute-start(bf16[2,192,48]{2,1,0:T(8,128)(2,1)S(1)} %pad_maximum_fusion.1), channel_id=1, source_target_pairs={{0,1},{1,0},{2,3},{3,2},{4,5},{5,4},{6,7},{7,6},{8,9},{9,8},{10,11... | collective-permute-start | bytes 110600 | tf_op jit(solution)/shard_map/ppermute | solution.py:523
  48.9 0.7 dynamic_slice.13
  49.6 0.7 dynamic_slice.12
  50.4 1.2 dynamic_slice.15
  51.6 0.7 pad_add_fusion.lens
  52.3 1.4 select_reduce_fusion.slots
  53.7 1.1 multiply_sine_fusion
  54.8 0.6 compare_convert_fusion
  55.5 1.3 broadcast_in_dim.30.gain_ref
  56.8 1.3 broadcast_in_dim.31.gain_ref
  58.0 92.9 %gather_kernel.1 = (bf16[8,2,96,4096]{3,2,1,0:T(8,128)(2,1)}, bf16[16,128,1536]{2,1,0:T(8,128)(2,1)}) custom-call(bf16[2,48,4096]{2,1,0:T(8,128)(2,1)} %bitcast.26, bf16[128,1536]{1,0:T(8,128)(2,1)} %tok_in.3), custom_call_target="tpu_custom_call" | custom-call | tf_op jit(solution)/shard_map/gather_kernel/pallas_call | solution.py:164
  151.0 0.0 collective-permute-done
  151.0 0.0 copy-done
  151.1 0.2 concatenate.7
  151.2 33.9 %all_gather.15 = bf16[1536,288]{1,0:T(8,128)(2,1)S(1)} all-gather(bf16[192,288]{1,0:T(8,128)(2,1)S(1)} %concatenate.7), channel_id=1, replica_groups=mesh['req'=8,'mdl'=16] {'req'}, dimensions={0}, use_global_device_ids=true | all-gather | bytes 995328 | tf_op jit(solution)/shard_map/all_gather | solution.py:527
  185.1 1.3 copy.24
  186.5 20.9 %attend_kernel.1 = (bf16[4,96,512]{2,1,0:T(8,128)(2,1)}, bf16[2,48,2048]{2,1,0:T(8,128)(2,1)}) custom-call(s32[4]{0:T(128)} %select_reduce_fusion.slots, s32[5]{0:T(128)} %pad_add_fusion.lens, bf16[2048,1536]{1,0:T(8,128)(2,1)} %bitcast.34, bf16[1,1536]{1,0:T(2,128)(2,1)} %broadcast_in_dim.30.gain_ref, bf16[288,1536]{1,0:T(8,128)(2,1)} %bitcast.25, ...), custom_call_target="tpu_custom_call" | custom-call | flops 6000000000 | bytes 20000000 | tf_op jit(solution)/shard_map/attend_kernel/pallas_call | solution.py:270
  207.4 0.0 all-gather.4.cloned.1.call-done.wo_hbm
  207.4 0.0 all-gather.6.cloned.1.call-done
  207.4 53.2 %feed_kernel.1 = bf16[128,1536]{1,0:T(8,128)(2,1)} custom-call(bf16[4,96,512]{2,1,0:T(8,128)(2,1)} %get-tuple-element.8.att_in, bf16[128,1536]{1,0:T(8,128)(2,1)} %tok_in.3, bf16[1,1536]{1,0:T(2,128)(2,1)} %broadcast_in_dim.31.gain_ref, bf16[1536,1536]{1,0:T(8,128)(2,1)} %all-gather.4.cloned.1.call-done.wo_hbm, bf16[8,2,3,192,256]{4,3,2,1,0:T(8,128)(2,1)} %bitcast.24), custom_call_target="tpu_custom_call" | custom-call | tf_op jit(solution)/shard_map/feed_kernel/pallas_call | solution.py:470
  260.7 1.9 multiply_convert_fusion
  (5 shorter events, 0.1 us)
Async XLA Ops:
  7.2 143.9 %copy-start = (bf16[192,96]{1,0:T(8,128)(2,1)S(1)}, bf16[192,96]{1,0:T(8,128)(2,1)}, u32[]{:S(2)}) copy-start(bf16[192,96]{1,0:T(8,128)(2,1)} %param.17) | copy-start | bytes 110596
  7.2 200.2 %all-gather.4.cloned.1.call-start = ((), (), s32[]{:S(2)}) async-start(), calls=%async_computation | async-start | bytes 5013504 | tf_op jit(solution)/shard_map/all_gather | solution.py:538
  38.9 168.5 %all-gather.6.cloned.1.call-start = ((), (), s32[]{:S(2)}) async-start(), calls=%async_computation.1 | async-start | bytes 5013504 | tf_op jit(solution)/shard_map/all_gather | solution.py:534
  42.5 108.5 %collective-permute-start = (bf16[2,192,48]{2,1,0:T(8,128)(2,1)S(1)}, bf16[2,192,48]{2,1,0:T(8,128)(2,1)S(1)}, u32[]{:S(2)}, u32[]{:S(2)}) collective-permute-start(bf16[2,192,48]{2,1,0:T(8,128)(2,1)S(1)} %pad_maximum_fusion.1), channel_id=1, source_target_pairs={{0,1},{1,0},{2,3},{3,2},{4,5},{5,4},{6,7},{7,6},{8,9},{9,8},{10,11... | collective-permute-start | bytes 110600 | tf_op jit(solution)/shard_map/ppermute | solution.py:523
Sparse Core Ops, SparseCore 0:
  39.0 60.1 all-gather.3
  101.4 62.8 all-gather.5

commit v2 on v1

--- a/solution.py
+++ b/solution.py
@@ -3,6 +3,7 @@
 
 import jax
 import jax.numpy as jnp
+import numpy as np
 from jax import lax
 from jax.experimental import pallas as pl
 from jax.experimental.pallas import tpu as pltpu
@@ -23,13 +24,12 @@
     return req, mdl
 
 
-class Spread:
-    def __init__(self, own, block, piece, ring, pair, dev, partner, send, recv):
-        self.own, self.block, self.piece = own, block, piece
-        self.u, self.v, self.dev, self.partner = ring, pair, dev, partner
-        self.send, self.recv, self.made = send, recv, []
-
-    def copy(self, index, src, dst, device):
+class Hub:
+    def __init__(self, send, recv):
+        self.send, self.recv, self.made, self.pending = send, recv, [], []
+
+    def copy(self, src, dst, device, awaited=True):
+        index = len(self.made)
         made = pltpu.make_async_remote_copy(
             src_ref=src,
             dst_ref=dst,
@@ -40,68 +40,100 @@
         )
         made.start()
         self.made.append(made)
+        if not awaited:
+            self.pending.append(made)
         return made
 
-    def at(self, du, flip):
-        return self.block(lax.rem(self.u + du, 4), 1 - self.v if flip else self.v)
-
-    def ring_dev(self, du):
-        return self.dev(lax.rem(self.u + du, 4), self.v)
-
-    def start(self):
-        here = self.at(0, False)
-        self.pair_copy = self.copy(0, self.own, here, self.dev(self.u, 1 - self.v))
-        self.up = self.copy(1, self.own, here, self.ring_dev(1))
-        self.down = self.copy(2, self.own, here, self.ring_dev(3))
-        self.own_p = self.copy(3, self.own, here, self.partner)
-
-    def pair_arrived(self):
-        self.pair_copy.wait_recv()
-        other = self.at(0, True)
-        self.up2 = self.copy(4, other, other, self.ring_dev(1))
-        self.down2 = self.copy(5, other, other, self.ring_dev(3))
-        self.copy(6, other, other, self.partner)
-
-    def ring_arrived(self, flip):
-        base = 7 + 4 * flip
-        (self.up2 if flip else self.up).wait_recv()
-        low = self.at(3, flip)
-        a = self.copy(base, self.piece(low, 0), self.piece(low, 0), self.ring_dev(1))
-        (self.down2 if flip else self.down).wait_recv()
-        high = self.at(1, flip)
-        b = self.copy(base + 1, self.piece(high, 1), self.piece(high, 1), self.ring_dev(3))
-        self.copy(base + 2, low, low, self.partner)
-        self.copy(base + 3, high, high, self.partner)
-        if flip:
-            self.far2 = (a, b)
-        else:
-            self.far = (a, b)
-
-    def far_arrived(self, flip):
-        base = 15 + 2 * flip
-        for h, made in enumerate(self.far2 if flip else self.far):
+    def finish(self):
+        for made in self.pending:
             made.wait_recv()
-            place = self.piece(self.at(2, flip), h)
-            self.copy(base + h, place, place, self.partner)
-
-    def finish(self):
-        self.awaited = [
-            self.pair_copy, self.up, self.down, self.up2, self.down2, *self.far, *self.far2
-        ]
         for made in self.made:
             made.wait_send()
-        for made in self.made:
-            if all(made is not other for other in self.awaited):
-                made.wait_recv()
-
-
-SPREAD_SEMS = 19
-
-
-def gather_kernel(kv_in, tok_in, kv_out, tok_out, kv_send, kv_recv, tok_send, tok_recv, local_sem):
+
+
+class Ring:
+    def __init__(self, hub, region, piece, dev, u):
+        self.hub, self.region, self.piece, self.dev = hub, region, piece, dev
+        self.here, self.up_to, self.down_to, self.opposite = (
+            u, lax.rem(u + 1, 4), lax.rem(u + 3, 4), lax.rem(u + 2, 4)
+        )
+
+    def start(self, src=None):
+        block = self.region(self.here)
+        src = block if src is None else src
+        self.up = self.hub.copy(src, block, self.dev(self.up_to))
+        self.down = self.hub.copy(src, block, self.dev(self.down_to))
+
+    def arrive(self):
+        self.up.wait_recv()
+        low = self.piece(self.down_to, 0)
+        self.far_low = self.hub.copy(low, low, self.dev(self.up_to))
+        self.down.wait_recv()
+        high = self.piece(self.up_to, 1)
+        self.far_high = self.hub.copy(high, high, self.dev(self.down_to))
+
+    def finish(self):
+        self.far_low.wait_recv()
+        self.far_high.wait_recv()
+
+    def share(self, u, device):
+        block = self.region(u)
+        self.hub.copy(block, block, device, awaited=False)
+
+
+class Spread:
+    def __init__(self, hub, own, block, piece, u, v, dev, partner):
+        self.hub, self.own, self.partner = hub, own, partner
+        self.here, self.other = block(u, v), block(u, 1 - v)
+        self.pair_dev = dev(u, 1 - v)
+
+        def ring(w):
+            return Ring(
+                hub,
+                lambda p: block(p, w),
+                lambda p, h: piece(block(p, w), h),
+                lambda p: dev(p, v),
+                u,
+            )
+
+        self.rings = (ring(v), ring(1 - v))
+
+    def start_pair(self):
+        self.pair = self.hub.copy(self.own, self.here, self.pair_dev)
+
+    def start_ring(self):
+        self.rings[0].start(self.own)
+        self.hub.copy(self.own, self.here, self.partner, awaited=False)
+
+    def pair_arrived(self):
+        self.pair.wait_recv()
+        self.rings[1].start()
+        self.hub.copy(self.other, self.other, self.partner, awaited=False)
+
+    def ring_arrived(self, which):
+        ring = self.rings[which]
+        ring.arrive()
+        ring.share(ring.down_to, self.partner)
+        ring.share(ring.up_to, self.partner)
+
+    def far_arrived(self, which):
+        ring = self.rings[which]
+        ring.finish()
+        ring.share(ring.opposite, self.partner)
+
+
+SEMS = 96
+
+
+def gather_kernel(
+    kv_in, tok_in, wq_in, wk_in, wv_in, wo_in, wg_in, wu_in, wd_in,
+    kv_out, tok_out, wqkv_out, wo_out, wm_out,
+    pack, send, recv, local_sem,
+):
     req, mdl = places()
     x, yh = req // 2, lax.rem(req, 2)
     z, yl, core = mdl // 4, lax.rem(mdl // 2, 2), lax.rem(mdl, 2)
+    y = yh * 2 + yl
     partner = {"req": req, "mdl": z * 4 + yl * 2 + 1 - core}
     rows = pl.ds(pl.multiple_of(core * HALF, HALF), HALF)
 
@@ -111,83 +143,194 @@
     def tok_dev(u, v):
         return {"req": req, "mdl": u * 4 + v * 2 + core}
 
+    def x_dev(u):
+        return kv_dev(u, yh)
+
+    def y_dev(u):
+        return {"req": x * 2 + u // 2, "mdl": z * 4 + lax.rem(u, 2) * 2 + core}
+
+    def z_dev(u):
+        return tok_dev(u, yl)
+
+    keep = []
+
+    def store(src, dst):
+        made = pltpu.make_async_copy(src, dst, local_sem.at[len(keep)])
+        made.start()
+        keep.append(made)
+
+    for kind, ref in enumerate((wg_in, wu_in, wd_in)):
+        store(ref, wm_out.at[x, yh, yl, kind])
+    store(wo_in, wo_out.at[z, core, x, yh, yl])
+    store(kv_in, kv_out.at[req, :, rows, :])
+    store(tok_in, tok_out.at[mdl])
+    pack[:, 0:HD] = wq_in[...]
+    pack[:, HD : HD + HALF] = jnp.transpose(wk_in[...])
+    pack[:, HD + HALF : 2 * HD] = jnp.transpose(wv_in[...])
+
     barrier = pltpu.get_barrier_semaphore()
-    peers = [
-        partner,
-        kv_dev(x, 1 - yh),
-        kv_dev(lax.rem(x + 1, 4), yh),
-        kv_dev(lax.rem(x + 3, 4), yh),
-        tok_dev(z, 1 - yl),
-        tok_dev(lax.rem(z + 1, 4), yl),
-        tok_dev(lax.rem(z + 3, 4), yl),
+    peers = [partner, kv_dev(x, 1 - yh)] + [
+        dev(lax.rem(place + step, 4))
+        for dev, place in ((x_dev, x), (y_dev, y), (z_dev, z))
+        for step in (1, 3)
     ]
     for peer in peers:
         pl.semaphore_signal(barrier, inc=1, device_id=peer, device_id_type=MESH)
     pl.semaphore_wait(barrier, len(peers))
 
+    hub = Hub(send, recv)
     kv = Spread(
-        kv_in,
+        hub, kv_in,
         lambda u, v: kv_out.at[u * 2 + v, :, rows, :],
         lambda ref, h: ref.at[h],
-        x, yh, kv_dev, partner, kv_send, kv_recv,
+        x, yh, kv_dev, partner,
     )
     tok = Spread(
-        tok_in,
+        hub, tok_in,
         lambda u, v: tok_out.at[u * 4 + v * 2 + core],
         lambda ref, h: ref.at[pl.ds(64 * h, 64)],
-        z, yl, tok_dev, partner, tok_send, tok_recv,
-    )
-    tok.start()
-    kv.start()
-    keep_kv = pltpu.make_async_copy(kv_in, kv.at(0, False), local_sem.at[0])
-    keep_tok = pltpu.make_async_copy(tok_in, tok.at(0, False), local_sem.at[1])
-    keep_kv.start()
-    keep_tok.start()
+        z, yl, tok_dev, partner,
+    )
+    qkv = Spread(
+        hub, pack,
+        lambda u, v: wqkv_out.at[u * 2 + v, core],
+        lambda ref, h: ref.at[pl.ds(96 * h, 96)],
+        x, yh, kv_dev, partner,
+    )
+    wo_x = Ring(
+        hub,
+        lambda u: wo_out.at[z, core, u, yh, yl],
+        lambda u, h: wo_out.at[z, core, u, yh, yl, pl.ds(48 * h, 48)],
+        x_dev, x,
+    )
+    wo_y = Ring(
+        hub,
+        lambda u: wo_out.at[z, core, :, u // 2, lax.rem(u, 2)],
+        lambda u, h: wo_out.at[z, core, pl.ds(2 * h, 2), u // 2, lax.rem(u, 2)],
+        y_dev, y,
+    )
+    wo_z = Ring(
+        hub,
+        lambda u: wo_out.at[u, core],
+        lambda u, h: wo_out.at[u, core, pl.ds(2 * h, 2)],
+        z_dev, z,
+    )
+    wm_x = Ring(
+        hub,
+        lambda u: wm_out.at[u, yh, yl],
+        lambda u, h: wm_out.at[u, yh, yl, :, pl.ds(96 * h, 96)],
+        x_dev, x,
+    )
+
+    def wm_ring(step):
+        u_x = lax.rem(x + step, 4)
+        return Ring(
+            hub,
+            lambda u: wm_out.at[u_x, u // 2, lax.rem(u, 2)],
+            lambda u, h: wm_out.at[u_x, u // 2, lax.rem(u, 2), :, pl.ds(96 * h, 96)],
+            y_dev, y,
+        )
+
+    wm_y = [wm_ring(step) for step in range(4)]
+
+    kv.start_pair()
+    tok.start_pair()
+    for made in keep[:4]:
+        made.wait()
+    wm_x.start()
+    wo_x.start(wo_in)
+    qkv.start_pair()
+    qkv.start_ring()
+    tok.start_ring()
+    wm_y[0].start()
+    kv.start_ring()
+    store(pack, wqkv_out.at[req, core])
+
+    wm_x.arrive()
+    wm_y[3].start()
+    wm_y[1].start()
+    wo_x.arrive()
     tok.pair_arrived()
-    tok.ring_arrived(False)
-    kv.ring_arrived(False)
-    tok.ring_arrived(True)
+    qkv.ring_arrived(0)
+    qkv.pair_arrived()
+    tok.ring_arrived(0)
+    wo_x.finish()
+    wo_y.start()
+    kv.ring_arrived(0)
+    wm_x.finish()
+    wm_y[2].start()
     kv.pair_arrived()
-    tok.far_arrived(False)
-    tok.far_arrived(True)
-    kv.far_arrived(False)
-    kv.ring_arrived(True)
-    kv.far_arrived(True)
-    keep_kv.wait()
-    keep_tok.wait()
-    tok.finish()
-    kv.finish()
-
-
-def gather(kv_own, tokens):
-    width = tokens.shape[1]
+    wm_y[0].arrive()
+    tok.ring_arrived(1)
+    qkv.far_arrived(0)
+    qkv.ring_arrived(1)
+    wo_y.arrive()
+    tok.far_arrived(0)
+    kv.far_arrived(0)
+    wo_y.finish()
+    wo_z.start()
+    wo_z.share(z, partner)
+    wm_y[3].arrive()
+    wm_y[1].arrive()
+    tok.far_arrived(1)
+    qkv.far_arrived(1)
+    kv.ring_arrived(1)
+    wo_z.arrive()
+    wo_z.share(wo_z.down_to, partner)
+    wo_z.share(wo_z.up_to, partner)
+    wm_y[2].arrive()
+    wo_z.finish()
+    wo_z.share(wo_z.opposite, partner)
+    kv.far_arrived(1)
+    for ring in wm_y:
+        ring.finish()
+    for made in keep[4:]:
+        made.wait()
+    hub.finish()
+
+
+def gather(kv_own, tokens, w_query, w_key, w_value, w_out, w_gate, w_up, w_down):
+    rows, width = tokens.shape
+    shape = lambda *dims: jax.ShapeDtypeStruct(dims, jnp.bfloat16)
     return pl.pallas_call(
         gather_kernel,
         out_shape=(
-            jax.ShapeDtypeStruct((8, 2, HD, kv_own.shape[2]), jnp.bfloat16),
-            jax.ShapeDtypeStruct((16, tokens.shape[0], width), jnp.bfloat16),
+            shape(8, 2, HD, kv_own.shape[2]),
+            shape(16, rows, width),
+            shape(8, 2, 192, 192),
+            shape(4, 2, 4, 2, 2, 96, 192),
+            shape(4, 2, 2, 3, 192, 256),
         ),
-        in_specs=[pl.BlockSpec(memory_space=pltpu.VMEM)] * 2,
-        out_specs=[pl.BlockSpec(memory_space=pl.ANY)] * 2,
-        scratch_shapes=[pltpu.SemaphoreType.DMA((SPREAD_SEMS,))] * 4
-        + [pltpu.SemaphoreType.DMA((2,))],
+        in_specs=[pl.BlockSpec(memory_space=pltpu.VMEM)] * 9,
+        out_specs=[pl.BlockSpec(memory_space=pl.ANY)] * 5,
+        scratch_shapes=[
+            pltpu.VMEM((192, 192), jnp.bfloat16),
+            pltpu.SemaphoreType.DMA((SEMS,)),
+            pltpu.SemaphoreType.DMA((SEMS,)),
+            pltpu.SemaphoreType.DMA((8,)),
+        ],
         compiler_params=pltpu.CompilerParams(collective_id=0, has_side_effects=True),
         name="gather_kernel",
-    )(kv_own, tokens)
+    )(kv_own, tokens, w_query, w_key, w_value, w_out, w_gate, w_up, w_down)
 
 
 def attend_kernel(
-    slots, lens, tok_ref, gain_ref, w_ref, cos_ref, sin_ref, kv_ref, att_ref, cache_ref, kv_width
+    lengths, member, owners, place,
+    tok_ref, gain_ref, w_ref, cos_ref, sin_ref, kv_ref, att_ref, cache_ref, kv_width,
 ):
-    request = pl.program_id(0)
-    length = lens[request]
-    core = lens[4]
+    length = lengths[place[0] * 4 + pl.program_id(0)]
+    core = place[1]
+    width = tok_ref.shape[1]
     numbers = tok_ref[...].astype(jnp.float32)
     scale = lax.rsqrt(jnp.mean(numbers * numbers, axis=-1, keepdims=True) + norm_eps)
     normed = (numbers * scale * gain_ref[...].astype(jnp.float32)).astype(jnp.bfloat16)
-    projected = lax.dot_general(
-        w_ref[...], normed, (((1,), (1,)), ((), ())), preferred_element_type=jnp.float32
-    )
+    halves = [
+        jnp.transpose(
+            jnp.dot(normed, w_ref[:, c].reshape(width, 192), preferred_element_type=jnp.float32)
+        )
+        for c in range(2)
+    ]
+    first = core == 0
     cosine, sine = cos_ref[...], sin_ref[...]
 
     def rotate(block):
@@ -196,13 +339,13 @@
             [low * cosine - high * sine, high * cosine + low * sine], axis=0
         )
 
-    query = jnp.transpose(rotate(projected[:HD])).astype(jnp.bfloat16)
-    keys_wide = rotate(projected[HD : 2 * HD])
-    values_wide = projected[2 * HD :]
+    query_raw = jnp.where(first, halves[0][:HD], halves[1][:HD])
+    query = jnp.transpose(rotate(query_raw)).astype(jnp.bfloat16)
+    keys_wide = rotate(jnp.concatenate([half[HD : HD + HALF] for half in halves], axis=0))
+    values_wide = jnp.concatenate([half[HD + HALF :] for half in halves], axis=0)
     keys = keys_wide.astype(jnp.bfloat16)
     values = values_wide.astype(jnp.bfloat16)
     live = (lax.broadcasted_iota(jnp.int32, (HALF, SUF), 1) < length).astype(jnp.float32)
-    first = core == 0
     cache_ref[0] = (
         jnp.where(first, keys_wide[:HALF], keys_wide[HALF:]) * live
     ).astype(jnp.bfloat16)
@@ -246,21 +389,25 @@
     att_ref[0] = jnp.transpose(summed / total).astype(jnp.bfloat16)
 
 
-def attend(slots, lens, tokens, gain, weights, cosine, sine, kv_all):
+def attend(lengths, member, owners, place, tokens, gain, weights, cosine, sine, kv_all):
     requests = 4
     width = tokens.shape[1]
     kv_width = kv_all.shape[3]
     whole = lambda r, *_: (0, 0)
+
+    def slot(r, lengths, member, owners, place):
+        return (owners[member[place[0] * 4 + r]], 0, 0, 0)
+
     spec = pltpu.PrefetchScalarGridSpec(
-        num_scalar_prefetch=2,
+        num_scalar_prefetch=4,
         grid=(requests,),
         in_specs=[
             pl.BlockSpec((SUF, width), lambda r, *_: (r, 0)),
             pl.BlockSpec((1, width), whole),
-            pl.BlockSpec(weights.shape, whole),
+            pl.BlockSpec(weights.shape, lambda r, *_: (0, 0, 0, 0)),
             pl.BlockSpec((HALF, SUF), whole),
             pl.BlockSpec((HALF, SUF), whole),
-            pl.BlockSpec((1, 2, HD, kv_width), lambda r, slots, lens: (slots[r], 0, 0, 0)),
+            pl.BlockSpec((1, 2, HD, kv_width), slot),
         ],
         out_specs=[
             pl.BlockSpec((1, HD, SUF), lambda r, *_: (r, 0, 0)),
@@ -281,7 +428,7 @@
             flops=6_000_000_000, bytes_accessed=20_000_000, transcendentals=10_000_000
         ),
         name="attend_kernel",
-    )(slots, lens, tokens, gain, weights, cosine, sine, kv_all)
+    )(lengths, member, owners, place, tokens, gain, weights, cosine, sine, kv_all)
 
 
 def feed_kernel(
@@ -304,12 +451,19 @@
             device_id={"req": req, "mdl": lax.rem(mdl + step, 16)},
             device_id_type=MESH,
         )
-    fetch = [pltpu.make_async_copy(wo_hbm, wo, w_sem.at[0])]
+    fetch = []
+    for u in range(4):
+        for c in range(2):
+            fetch.append(
+                pltpu.make_async_copy(
+                    wo_hbm.at[u, c], wo.at[:, :, u, :, c], w_sem.at[len(fetch)]
+                )
+            )
     for block in range(2):
         for kind in range(3):
             fetch.append(
                 pltpu.make_async_copy(
-                    wm_hbm.at[:, block, kind], wm.at[block, kind], w_sem.at[1 + 3 * block + kind]
+                    wm_hbm.at[:, :, block, kind], wm.at[block, kind], w_sem.at[len(fetch)]
                 )
             )
     for made in fetch:
@@ -346,13 +500,22 @@
     att[mdl] = att_in[z, :, columns]
     for made in exchange:
         made.wait_recv()
-    fetch[0].wait()
+    for made in fetch[:8]:
+        made.wait()
     width = tok_in.shape[1]
     attended = jnp.transpose(att[...].reshape(16 * HD, 128))
     own_rows = rows_all.at[z, core]
-    for column in range(0, width, 512):
-        here = slice(column, column + 512)
-        attention = jnp.dot(attended, wo[:, here], preferred_element_type=jnp.float32)
+    for u in range(4):
+        attention = jnp.concatenate(
+            [
+                jnp.dot(
+                    attended, wo[u, v].reshape(16 * HD, 192), preferred_element_type=jnp.float32
+                )
+                for v in range(2)
+            ],
+            axis=1,
+        )
+        here = slice(384 * u, 384 * u + 384)
         own_rows[:, here] = (tok_in[:, here].astype(jnp.float32) + attention).astype(jnp.bfloat16)
 
     made = []
@@ -365,7 +528,7 @@
     up = go(own_rows, own_rows, peer(1), 0)
     down = go(own_rows, own_rows, peer(3), 1)
     across = go(own_rows, own_rows, peer(0, True), 2)
-    for copy in fetch[1:]:
+    for copy in fetch[8:]:
         copy.wait()
 
     def feed(slot, du):
@@ -474,8 +637,8 @@
         out_specs=vmem,
         scratch_shapes=[
             pltpu.VMEM((16, HD, 128), bf16),
-            pltpu.VMEM((width, width), bf16),
-            pltpu.VMEM((2, 3, 8, 192, 256), bf16),
+            pltpu.VMEM((4, 2, 4, 2, 2, HD, 192), bf16),
+            pltpu.VMEM((2, 3, 4, 2, 192, 256), bf16),
             pltpu.VMEM((4, 2, rows, width), bf16),
             pltpu.VMEM((4, 2, rows, width), bf16),
             pltpu.VMEM((4, rows, width), bf16),
@@ -488,7 +651,7 @@
             pltpu.SemaphoreType.DMA((15,)),
             pltpu.SemaphoreType.DMA((19,)),
             pltpu.SemaphoreType.DMA((19,)),
-            pltpu.SemaphoreType.DMA((7,)),
+            pltpu.SemaphoreType.DMA((14,)),
         ],
         compiler_params=pltpu.CompilerParams(
             collective_id=1, has_side_effects=True, vmem_limit_bytes=60 << 20
@@ -514,55 +677,38 @@
     owners,
 ):
     req, mdl = places()
-    core = mdl % 2
-    low_half = core == 0
     prefix_length = prefix_cache.shape[2]
-    kv_own = prefix_cache[:, 0].transpose(0, 2, 1)
-    own_kv = jnp.stack([w_key, w_value], axis=0)
-    swap = [(m, m ^ 1) for m in range(16)]
-    other_kv = lax.ppermute(own_kv, "mdl", swap)
-    even = jnp.where(low_half, own_kv, other_kv)
-    odd = jnp.where(low_half, other_kv, own_kv)
-    packed = jnp.concatenate([w_query, even[0], odd[0], even[1], odd[1]], axis=1)
-    w_qkv = lax.all_gather(packed, "req", axis=0, tiled=True).T
-    mlp_own = jnp.stack([w_gate, w_up, w_down.T], axis=0)
-    groups = [
-        [r * 16 + z * 4 + y * 2 + c for r in range(8) for y in range(2)]
-        for z in range(4)
-        for c in range(2)
-    ]
-    w_mlp = lax.all_gather(mlp_own, ("req", "mdl"), axis_index_groups=groups).reshape(
-        8, 2, 3, 192, 256
-    )
-    w_out_rows = lax.all_gather(w_out, "req", axis=1, tiled=True)
-    w_out_all = lax.all_gather(w_out_rows, "mdl", axis=0, tiled=True)
-
-    kv_all, tok_all = gather(kv_own, tokens)
-
-    half = HD // 2
-    frequency = rope_base ** (-(jnp.arange(half).astype(jnp.float32) * 2.0 / HD))
-    positions = (jnp.arange(SUF, dtype=jnp.int32) + prefix_length).astype(jnp.float32)
-    angles = positions[:, None] * frequency[None, :]
-    local_lengths = lax.dynamic_slice_in_dim(lengths, req * 4, 4)
-    local_members = lax.dynamic_slice_in_dim(member, req * 4, 4)
-    group_numbers = jnp.arange(owners.shape[0], dtype=jnp.int32)
-    slots = jnp.sum(
-        jnp.where(local_members[:, None] == group_numbers[None, :], owners[None, :], 0), axis=1
-    )
-    lens = jnp.concatenate([local_lengths, core[None].astype(jnp.int32)])
+    kv_all, tok_all, w_qkv, w_out_all, w_mlp = gather(
+        prefix_cache[:, 0].transpose(0, 2, 1),
+        tokens,
+        w_query,
+        w_key.T,
+        w_value.T,
+        w_out,
+        w_gate,
+        w_up,
+        w_down.T,
+    )
+    half = np.arange(HD // 2).astype(np.float32)
+    frequency = np.float32(rope_base) ** (-(half * np.float32(2.0) / np.float32(HD)))
+    positions = (np.arange(SUF) + prefix_length).astype(np.float32)
+    angles = (frequency[:, None] * positions[None, :]).astype(np.float64)
+    place = jnp.stack([req, mdl % 2]).astype(jnp.int32)
     att, cache = attend(
-        slots,
-        lens,
+        lengths,
+        member,
+        owners,
+        place,
         tok_all.reshape(16 * tokens.shape[0], tokens.shape[1]),
         attention_gain[None, :],
         w_qkv,
-        jnp.cos(angles).T,
-        jnp.sin(angles).T,
+        np.cos(angles).astype(np.float32),
+        np.sin(angles).astype(np.float32),
         kv_all,
     )
     hidden = feed_forward(att, tokens, feed_gain[None, :], w_out_all, w_mlp)
     own_offset = (mdl % 4) * tokens.shape[0] + jnp.arange(tokens.shape[0], dtype=jnp.int32)
-    own_length = lax.dynamic_index_in_dim(local_lengths, mdl // 4, keepdims=False)
+    own_length = lax.dynamic_index_in_dim(lengths, req * 4 + mdl // 4, keepdims=False)
     own_valid = own_offset < own_length
     hidden = (hidden.astype(jnp.float32) * own_valid[:, None].astype(jnp.float32)).astype(
         jnp.bfloat16

time: 270 us -> 181 us (0.67)
  blocking collectives: 63.8 us -> 0 us
  between operations: 14.1 us -> 0.71 us
  local copies, waits for them, and re-layouts: 10.3 us -> 2.48 us
  Pallas kernels: 167 us -> 174 us
  starting transfers between devices: 6.51 us -> 0 us
  other arithmetic: 7.53 us -> 3.16 us
    all_gather x2 -> x0, blocking collectives: 63.8 us -> none  [the longest x1 33.9 us: local(): w_qkv = lax.all_gather(packed, 'req', axis=0, tiled=True).T]
    pallas_call x1, Pallas kernels: 92.9 us -> 105 us  [gather(): pl.pallas_call(gather_kernel, out_shape=(shape(8, 2, HD, kv_own.shape[2])...]
    pallas_call x1, Pallas kernels: 53.2 us -> 46.4 us  [feed_forward(): pl.pallas_call(feed_kernel, out_shape=jax.ShapeDtypeStruct((rows, width),...]
    ppermute x1 -> x0, starting transfers between devices: 6.43 us -> none  [local(): other_kv = lax.ppermute(own_kv, 'mdl', swap)]
  transfers between devices with their start and end apart: 3 -> 0, of which waited for: 0 -> 0; matrix products, arithmetic and copies ran while one was open for 5% -> 0% of each run, Pallas kernels for 42% -> 0%
where the time goes in v2:
time: 181 us
  Pallas kernels  174 us (96%)
  other arithmetic  3.16 us (2%)
  local copies, waits for them, and re-layouts  2.48 us (1%)
    pallas_call x1, Pallas kernels, gather(): pl.pallas_call(gather_kernel, out_shape=(shape(8, 2, HD, kv_own.shape[2])...  105 us
    pallas_call x1, Pallas kernels, feed_forward(): pl.pallas_call(feed_kernel, out_shape=jax.ShapeDtypeStruct((rows, width),...  46.4 us
    pallas_call x1, Pallas kernels, attend(): pl.pallas_call(functools.partial(attend_kernel, kv_width=kv_width), grid_...  23.1 us

profile of v2, /device:TPU:1, one launch (start us, length us, event | category | flops | bytes accessed | tf_op | source)
XLA Modules:
  0.0 180.6 jit_solution(14545202854174887118)
XLA Ops:
  0.6 0.6 pad_add_fusion.place
  1.3 104.8 %gather_kernel.1 = (bf16[8,2,96,4096]{3,2,1,0:T(8,128)(2,1)}, bf16[16,128,1536]{2,1,0:T(8,128)(2,1)}, bf16[8,2,192,192]{3,2,1,0:T(8,128)(2,1)}, bf16[4,2,4,2,2,9...) custom-call(bf16[2,48,4096]{2,1,0:T(8,128)(2,1)} %bitcast.11, bf16[128,1536]{1,0:T(8,128)(2,1)} %tok_in.3, ...), custom_call_target="tpu_custom_call" | custom-call | tf_op jit(solution)/shard_map/gather_kernel/pallas_call | solution.py:295
  106.1 1.3 broadcast_in_dim.7.gain_ref
  107.4 0.0 copy-start
  107.4 23.1 %attend_kernel.1 = (bf16[4,96,512]{2,1,0:T(8,128)(2,1)}, bf16[2,48,2048]{2,1,0:T(8,128)(2,1)}) custom-call(s32[32]{0:T(128)} %lengths.1, s32[32]{0:T(128)} %member.1, s32[8]{0:T(128)} %owners.1, s32[2]{0:T(128)} %pad_add_fusion.place, bf16[2048,1536]{1,0:T(8,128)(2,1)} %bitcast.15, bf16[1,1536]{1,0:T(2,128)(2,1)} %broadcast_in_dim.7.gain_ref, ...), custom_call_target="tpu_custom_call" | custom-call | flops 6000000000 | bytes 20000000 | tf_op jit(solution)/shard_map/attend_kernel/pallas_call | solution.py:417
  130.5 0.0 copy-start.1
  130.5 0.0 copy-done
  130.5 0.6 broadcast_in_dim.8.gain_ref
  131.1 46.4 %feed_kernel.1 = bf16[128,1536]{1,0:T(8,128)(2,1)} custom-call(bf16[4,96,512]{2,1,0:T(8,128)(2,1)} %get-tuple-element.12.att_in, bf16[128,1536]{1,0:T(8,128)(2,1)} %tok_in.3, bf16[1,1536]{1,0:T(2,128)(2,1)} %broadcast_in_dim.8.gain_ref, bf16[4,2,4,2,2,96,192]{6,5,4,3,2,1,0:T(8,128)(2,1)} %get-tuple-element.13.wo_hbm, ...), custom_call_target="tpu_custom_call" | custom-call | tf_op jit(solution)/shard_map/feed_kernel/pallas_call | solution.py:633
  177.5 0.0 copy-done.1
  177.5 0.6 dynamic_slice.4
  178.1 0.6 compare_convert_fusion
  178.7 1.9 %multiply_convert_fusion = bf16[128,1536]{1,0:T(8,128)(2,1)} fusion(bf16[128,1536]{1,0:T(8,128)(2,1)} %feed_kernel.1, f32[128]{0:T(128)S(1)} %compare_convert_fusion), kind=kLoop, calls=%fused_computation | loop fusion | flops 589824 | bytes 786944 | tf_op jit(solution)/shard_map/convert_element_type | solution.py:713
Async XLA Ops:
  107.4 23.1 %copy-start = (bf16[1536]{0:T(1024)(128)(2,1)S(1)}, bf16[1536]{0:T(1024)(128)(2,1)}, u32[]{:S(2)}) copy-start(bf16[1536]{0:T(1024)(128)(2,1)} %param.18) | copy-start | bytes 9220
  130.5 47.0 %copy-start.1 = (s32[32]{0:T(128)S(1)}, s32[32]{0:T(128)}, u32[]{:S(2)}) copy-start(s32[32]{0:T(128)} %lengths.1) | copy-start | bytes 388

commit v3 on v2

v3 whole, which is shorter than its diff:
```python
import math

import jax
import jax.numpy as jnp
import numpy as np
from jax import lax
from jax.experimental import pallas as pl
from jax.experimental.pallas import tpu as pltpu
from jax.sharding import PartitionSpec as P

HD = 96
HALF = 48
SUF = 512
rope_base = 100000.0
norm_eps = 1e-05
MESH = pl.DeviceIdType.MESH
LOG2E = 1.4426950408889634


def places():
    req = lax.axis_index("req")
    mdl = lax.axis_index("mdl")
    return req, mdl


class Hub:
    def __init__(self, send, recv):
        self.send, self.recv, self.made, self.pending = send, recv, [], []

    def copy(self, src, dst, device, awaited=True):
        index = len(self.made)
        made = pltpu.make_async_remote_copy(
            src_ref=src,
            dst_ref=dst,
            send_sem=self.send.at[index],
            recv_sem=self.recv.at[index],
            device_id=device,
            device_id_type=MESH,
        )
        made.start()
        self.made.append(made)
        if not awaited:
            self.pending.append(made)
        return made

    def shared(self):
        for made in self.pending:
            made.wait_recv()
        self.pending = []

    def finish(self):
        self.shared()
        for made in self.made:
            made.wait_send()


class Ring:
    def __init__(self, hub, region, piece, dev, u):
        self.hub, self.region, self.piece, self.dev = hub, region, piece, dev
        self.here, self.up_to, self.down_to, self.opposite = (
            u, lax.rem(u + 1, 4), lax.rem(u + 3, 4), lax.rem(u + 2, 4)
        )

    def start(self, src=None):
        block = self.region(self.here)
        src = block if src is None else src
        self.up = self.hub.copy(src, block, self.dev(self.up_to))
        self.down = self.hub.copy(src, block, self.dev(self.down_to))

    def arrive(self):
        self.up.wait_recv()
        low = self.piece(self.down_to, 0)
        self.far_low = self.hub.copy(low, low, self.dev(self.up_to))
        self.down.wait_recv()
        high = self.piece(self.up_to, 1)
        self.far_high = self.hub.copy(high, high, self.dev(self.down_to))

    def finish(self):
        self.far_low.wait_recv()
        self.far_high.wait_recv()

    def share(self, u, device):
        block = self.region(u)
        return self.hub.copy(block, block, device, awaited=False)


class Spread:
    def __init__(self, hub, own, block, piece, u, v, dev, partner):
        self.hub, self.own, self.partner = hub, own, partner
        self.here, self.other = block(u, v), block(u, 1 - v)
        self.pair_dev = dev(u, 1 - v)
        self.handed = []

        def ring(w):
            return Ring(
                hub,
                lambda p: block(p, w),
                lambda p, h: piece(block(p, w), h),
                lambda p: dev(p, v),
                u,
            )

        self.rings = (ring(v), ring(1 - v))

    def start_pair(self):
        self.pair = self.hub.copy(self.own, self.here, self.pair_dev)

    def start_ring(self):
        self.rings[0].start(self.own)
        self.handed.append(self.hub.copy(self.own, self.here, self.partner))

    def pair_arrived(self):
        self.pair.wait_recv()
        self.rings[1].start()
        self.handed.append(self.hub.copy(self.other, self.other, self.partner))

    def ring_arrived(self, which):
        ring = self.rings[which]
        ring.arrive()
        self.hand(ring, ring.down_to)
        self.hand(ring, ring.up_to)

    def far_arrived(self, which):
        ring = self.rings[which]
        ring.finish()
        self.hand(ring, ring.opposite)

    def hand(self, ring, u):
        block = ring.region(u)
        self.handed.append(self.hub.copy(block, block, self.partner))

    def shared(self):
        for made in self.handed:
            made.wait_recv()


SEMS = 116


def layer_kernel(
    lengths, member, owners,
    kv_in, tok_in, wq_in, wk_in, wv_in, wo_in, wg_in, wu_in, wd_in,
    gain_ref, feed_gain_ref, cos_ref, sin_ref,
    out_ref, cache_ref,
    kv_all, tok_all, wqkv, wo, wm, pack, query, keys, values, att_out, att,
    rows_all, part, from_pair, sums, relay, plain, joined, to_relay,
    send, recv, a2a_send, a2a_recv, local_sem,
):
    req, mdl = places()
    x, yh = req // 2, lax.rem(req, 2)
    z, yl, core = mdl // 4, lax.rem(mdl // 2, 2), lax.rem(mdl, 2)
    y = yh * 2 + yl
    quarter = lax.rem(mdl, 4)
    width = tok_in.shape[1]
    partner = {"req": req, "mdl": z * 4 + yl * 2 + 1 - core}
    rows = pl.ds(pl.multiple_of(core * HALF, HALF), HALF)

    def kv_dev(u, v):
        return {"req": u * 2 + v, "mdl": mdl}

    def tok_dev(u, v):
        return {"req": req, "mdl": u * 4 + v * 2 + core}

    def x_dev(u):
        return kv_dev(u, yh)

    def y_dev(u):
        return {"req": x * 2 + u // 2, "mdl": z * 4 + lax.rem(u, 2) * 2 + core}

    def z_dev(u):
        return tok_dev(u, yl)

    barrier = pltpu.get_barrier_semaphore()
    peers = [kv_dev(x, 1 - yh)]
    peers += [x_dev(lax.rem(x + step, 4)) for step in (1, 3)]
    peers += [y_dev(lax.rem(y + step, 4)) for step in (1, 3)]
    peers += [{"req": req, "mdl": lax.rem(mdl + step, 16)} for step in range(1, 16)]
    for peer in peers:
        pl.semaphore_signal(barrier, inc=1, device_id=peer, device_id_type=MESH)

    keep = []

    def store(src, dst):
        made = pltpu.make_async_copy(src, dst, local_sem.at[len(keep)])
        made.start()
        keep.append(made)

    store(wo_in, wo.at[z, core, x, yh, yl])
    for kind, ref in enumerate((wg_in, wu_in, wd_in)):
        store(ref, wm.at[x, yh, yl, kind])
    store(kv_in, kv_all.at[req, :, rows, :])
    store(tok_in, tok_all.at[mdl])
    pack[:, 0:HD] = wq_in[...]
    pack[:, HD : HD + HALF] = jnp.transpose(wk_in[...])
    pack[:, HD + HALF : 2 * HD] = jnp.transpose(wv_in[...])
    pl.semaphore_wait(barrier, len(peers))

    hub = Hub(send, recv)
    kv = Spread(
        hub, kv_in,
        lambda u, v: kv_all.at[u * 2 + v, :, rows, :],
        lambda ref, h: ref.at[h],
        x, yh, kv_dev, partner,
    )
    tok = Spread(
        hub, tok_in,
        lambda u, v: tok_all.at[u * 4 + v * 2 + core],
        lambda ref, h: ref.at[pl.ds(64 * h, 64)],
        z, yl, tok_dev, partner,
    )
    qkv = Spread(
        hub, pack,
        lambda u, v: wqkv.at[u * 2 + v, core],
        lambda ref, h: ref.at[pl.ds(96 * h, 96)],
        x, yh, kv_dev, partner,
    )
    wo_x = Ring(
        hub,
        lambda u: wo.at[z, core, u, yh, yl],
        lambda u, h: wo.at[z, core, u, yh, yl, pl.ds(48 * h, 48)],
        x_dev, x,
    )
    wo_y = Ring(
        hub,
        lambda u: wo.at[z, core, :, u // 2, lax.rem(u, 2)],
        lambda u, h: wo.at[z, core, pl.ds(2 * h, 2), u // 2, lax.rem(u, 2)],
        y_dev, y,
    )
    wo_z = Ring(
        hub,
        lambda u: wo.at[u, core],
        lambda u, h: wo.at[u, core, pl.ds(2 * h, 2)],
        z_dev, z,
    )
    wm_x = Ring(
        hub,
        lambda u: wm.at[u, yh, yl],
        lambda u, h: wm.at[u, yh, yl, :, pl.ds(96 * h, 96)],
        x_dev, x,
    )

    def wm_ring(step):
        u_x = lax.rem(x + step, 4)
        return Ring(
            hub,
            lambda u: wm.at[u_x, u // 2, lax.rem(u, 2)],
            lambda u, h: wm.at[u_x, u // 2, lax.rem(u, 2), :, pl.ds(96 * h, 96)],
            y_dev, y,
        )

    wm_y = [wm_ring(step) for step in range(4)]

    def project(r, carry):
        numbers = tok_all[pl.ds(4 * r, 4)].reshape(SUF, width).astype(jnp.float32)
        scale = lax.rsqrt(jnp.mean(numbers * numbers, axis=-1, keepdims=True) + norm_eps)
        normed = (numbers * scale * gain_ref[...].astype(jnp.float32)).astype(jnp.bfloat16)
        halves = [
            jnp.transpose(
                jnp.dot(
                    normed, wqkv[:, c].reshape(width, 192), preferred_element_type=jnp.float32
                )
            )
            for c in range(2)
        ]
        cosine, sine = cos_ref[...], sin_ref[...]

        def rotate(block):
            low, high = block[:HALF], block[HALF:]
            return jnp.concatenate(
                [low * cosine - high * sine, high * cosine + low * sine], axis=0
            )

        first = core == 0
        query_raw = jnp.where(first, halves[0][:HD], halves[1][:HD])
        keys_wide = rotate(jnp.concatenate([half[HD : HD + HALF] for half in halves], axis=0))
        values_wide = jnp.concatenate([half[HD + HALF :] for half in halves], axis=0)
        query[r] = jnp.transpose(rotate(query_raw)).astype(jnp.bfloat16)
        keys[r] = keys_wide.astype(jnp.bfloat16)
        values[r] = values_wide.astype(jnp.bfloat16)
        length = lengths[req * 4 + r]
        live = (lax.broadcasted_iota(jnp.int32, (HALF, SUF), 1) < length).astype(jnp.float32)
        columns = pl.ds(pl.multiple_of(r * SUF, SUF), SUF)
        for kind, wide in enumerate((keys_wide, values_wide)):
            own = jnp.where(first, wide[:HALF], wide[HALF:])
            cache_ref[kind, :, columns] = (own * live).astype(jnp.bfloat16)
        return carry

    def attend(i, carry):
        r = lax.rem(z + 1 + i, 4)
        length = lengths[req * 4 + r]
        slot = owners[member[req * 4 + r]]
        factor = LOG2E / math.sqrt(HD)
        chunk = 1024
        top = total = summed = None
        for j in range(0, kv_all.shape[3] + 1, chunk):
            own = j == kv_all.shape[3]
            if own:
                key_part, value_part = keys[r], values[r]
            else:
                key_part = kv_all[slot, 0, :, j : j + chunk]
                value_part = kv_all[slot, 1, :, j : j + chunk]
            scores = jnp.dot(query[r], key_part, preferred_element_type=jnp.float32)
            if own:
                row = lax.broadcasted_iota(jnp.int32, scores.shape, 0)
                column = lax.broadcasted_iota(jnp.int32, scores.shape, 1)
                allowed = (column <= row) & (column < length)
                scores = jnp.where(allowed, scores, -1e30)
            part_top = jnp.max(scores, axis=-1, keepdims=True)
            new_top = part_top if top is None else jnp.maximum(top, part_top)
            weights = jnp.exp2((scores - new_top) * factor)
            if own:
                weights = jnp.where(allowed, weights, 0.0)
            part_total = jnp.sum(weights, axis=-1, keepdims=True)
            part_sum = lax.dot_general(
                weights.astype(jnp.bfloat16),
                value_part,
                (((1,), (1,)), ((), ())),
                preferred_element_type=jnp.float32,
            )
            if top is None:
                total, summed = part_total, part_sum
            else:
                carried = jnp.exp2((top - new_top) * factor)
                total = total * carried + part_total
                summed = summed * carried + part_sum
            top = new_top
        att_out[r] = jnp.transpose(summed / total).astype(jnp.bfloat16)
        for j in range(4):

            @pl.when(r * 4 + j != mdl)
            def _():
                pltpu.make_async_remote_copy(
                    src_ref=att_out.at[r, :, pl.ds(128 * j, 128)],
                    dst_ref=att.at[mdl],
                    send_sem=a2a_send.at[i * 4 + j],
                    recv_sem=a2a_recv.at[i * 4 + quarter],
                    device_id={"req": req, "mdl": r * 4 + j},
                    device_id_type=MESH,
                ).start()

        return carry

    wo_x.start(wo_in)
    qkv.start_ring()
    qkv.start_pair()
    tok.start_pair()
    tok.start_ring()
    store(pack, wqkv.at[req, core])
    wo_x.arrive()
    qkv.ring_arrived(0)
    qkv.pair_arrived()
    kv.start_ring()
    wo_x.finish()
    keep[0].wait()
    wo_y.start()
    kv.start_pair()
    for made in keep[1:4]:
        made.wait()
    wm_x.start()
    wm_y[0].start()
    tok.pair_arrived()
    tok.ring_arrived(0)
    qkv.far_arrived(0)
    wo_y.arrive()
    tok.ring_arrived(1)
    kv.ring_arrived(0)
    tok.far_arrived(0)
    tok.far_arrived(1)
    wm_x.arrive()
    wm_y[3].start()
    wm_y[1].start()
    kv.pair_arrived()
    qkv.ring_arrived(1)
    wo_y.finish()
    wo_z.start()
    wo_z.share(z, partner)
    qkv.far_arrived(1)
    wm_y[0].arrive()
    for made in keep[4:]:
        made.wait()
    tok.shared()
    qkv.shared()
    lax.fori_loop(0, 4, project, 0)
    kv.far_arrived(0)
    wo_z.arrive()
    wo_z.share(wo_z.down_to, partner)
    wo_z.share(wo_z.up_to, partner)
    wm_y[3].arrive()
    wm_y[1].arrive()
    kv.ring_arrived(1)
    wm_x.finish()
    wm_y[2].start()
    wo_z.finish()
    wo_z.share(wo_z.opposite, partner)
    kv.far_arrived(1)
    kv.shared()
    lax.fori_loop(0, 4, attend, 0)
    wm_y[2].arrive()
    att[mdl] = att_out[z, :, pl.ds(pl.multiple_of(quarter * 128, 128), 128)]

    def exchange(i, j, sending):
        k = i * 4 + j
        made = pltpu.make_async_remote_copy(
            src_ref=att_out.at[0, :, pl.ds(0, 128)],
            dst_ref=att.at[j],
            send_sem=a2a_send.at[k],
            recv_sem=a2a_recv.at[k],
            device_id=partner,
            device_id_type=MESH,
        )

        def wait():
            made.wait_send() if sending else made.wait_recv()

        if i < 3:
            wait()
        else:
            pl.when(quarter != j)(wait)

    hub.shared()
    for i in range(4):
        for j in range(4):
            exchange(i, j, False)
    attended = jnp.transpose(att[...].reshape(16 * HD, 128))
    own_rows = rows_all.at[z, core]
    for u in range(4):
        attention = jnp.concatenate(
            [
                jnp.dot(
                    attended,
                    jnp.concatenate(
                        [wo[k // 4, k % 2, u, v, (k // 2) % 2] for k in range(16)], axis=0
                    ),
                    preferred_element_type=jnp.float32,
                )
                for v in range(2)
            ],
            axis=1,
        )
        here = slice(384 * u, 384 * u + 384)
        own_rows[:, here] = (tok_in[:, here].astype(jnp.float32) + attention).astype(jnp.bfloat16)

    def peer(du, flip=False):
        other = 1 - core if flip else core
        return {"req": req, "mdl": lax.rem(z + du, 4) * 4 + yl * 2 + other}

    go = hub.copy
    up = go(own_rows, own_rows, peer(1))
    down = go(own_rows, own_rows, peer(3))
    across = go(own_rows, own_rows, peer(0, True))
    for ring in wm_y:
        ring.finish()

    def feed(slot, du):
        there = rows_all.at[lax.rem(z + du, 4)]
        numbers = there[...].reshape(256, width).astype(jnp.float32)
        scale = lax.rsqrt(jnp.mean(numbers * numbers, axis=-1, keepdims=True) + norm_eps)
        normed = (numbers * scale * feed_gain_ref[...].astype(jnp.float32)).astype(jnp.bfloat16)
        active = []
        for block in range(2):
            gate = jnp.dot(
                normed,
                wm[:, :, block, 0].reshape(width, 256),
                preferred_element_type=jnp.float32,
            )
            lift = jnp.dot(
                normed,
                wm[:, :, block, 1].reshape(width, 256),
                preferred_element_type=jnp.float32,
            )
            active.append((gate / (1.0 + jnp.exp(-gate)) * lift).astype(jnp.bfloat16))
        for u in range(4):
            parts = [
                lax.dot_general(
                    active[block],
                    wm[u, :, block, 2].reshape(384, 256),
                    (((1,), (1,)), ((), ())),
                    preferred_element_type=jnp.float32,
                )
                for block in range(2)
            ]
            part[slot, :, :, 384 * u : 384 * u + 384] = (
                (parts[0] + parts[1]).astype(jnp.bfloat16).reshape(2, 128, 384)
            )
        return go(part.at[slot, 1 - core], from_pair.at[slot], peer(0, True))

    def pair_sum(slot, copy):
        copy.wait_recv()
        sums[slot] = part[slot, core].astype(jnp.float32) + from_pair[slot].astype(jnp.float32)

    across.wait_recv()
    pair0 = feed(0, 0)
    up.wait_recv()
    low = rows_all.at[lax.rem(z + 3, 4), core]
    far_a = go(low.at[pl.ds(0, 64)], low.at[pl.ds(0, 64)], peer(1))
    low_p = go(low, low, peer(0, True))
    down.wait_recv()
    high = rows_all.at[lax.rem(z + 1, 4), core]
    far_b = go(high.at[pl.ds(64, 64)], high.at[pl.ds(64, 64)], peer(3))
    high_p = go(high, high, peer(0, True))
    low_p.wait_recv()
    pair3 = feed(3, 3)
    high_p.wait_recv()
    pair1 = feed(1, 1)
    far = rows_all.at[lax.rem(z + 2, 4), core]
    far_a.wait_recv()
    far_pa = go(far.at[pl.ds(0, 64)], far.at[pl.ds(0, 64)], peer(0, True))
    far_b.wait_recv()
    far_pb = go(far.at[pl.ds(64, 64)], far.at[pl.ds(64, 64)], peer(0, True))
    pair_sum(3, pair3)
    plain[0] = sums[3, 0:64].astype(jnp.bfloat16)
    plain_a = go(plain.at[0], plain.at[2], peer(3))
    pair_sum(1, pair1)
    plain[1] = sums[1, 64:128].astype(jnp.bfloat16)
    plain_b = go(plain.at[1], plain.at[3], peer(1))
    far_pa.wait_recv()
    far_pb.wait_recv()
    pair2 = feed(2, 2)
    pair_sum(2, pair2)
    to_relay[...] = sums[2].astype(jnp.bfloat16)
    relay_a = go(to_relay.at[pl.ds(0, 64)], relay.at[0], peer(1))
    relay_b = go(to_relay.at[pl.ds(64, 64)], relay.at[1], peer(3))
    pair_sum(0, pair0)
    relay_a.wait_recv()
    joined[0] = (sums[1, 0:64] + relay[0].astype(jnp.float32)).astype(jnp.bfloat16)
    joined_a = go(joined.at[0], joined.at[2], peer(1))
    relay_b.wait_recv()
    joined[1] = (sums[3, 64:128] + relay[1].astype(jnp.float32)).astype(jnp.bfloat16)
    joined_b = go(joined.at[1], joined.at[3], peer(3))
    plain_a.wait_recv()
    plain_b.wait_recv()
    joined_a.wait_recv()
    joined_b.wait_recv()
    for h in range(2):
        here = slice(64 * h, 64 * h + 64)
        feed_sum = (
            sums[0, here]
            + plain[2 + h].astype(jnp.float32)
            + joined[2 + h].astype(jnp.float32)
        )
        out_ref[here, :] = (own_rows[here, :].astype(jnp.float32) + feed_sum).astype(jnp.bfloat16)
    for i in range(4):
        for j in range(4):
            exchange(i, j, True)
    hub.finish()


def layer(scalars, arrays):
    kv_own, tokens = arrays[:2]
    rows, width = tokens.shape
    bf16, f32 = jnp.bfloat16, jnp.float32
    vmem = pl.BlockSpec(memory_space=pltpu.VMEM)
    return pl.pallas_call(
        layer_kernel,
        out_shape=(
            jax.ShapeDtypeStruct((rows, width), bf16),
            jax.ShapeDtypeStruct((2, HALF, 4 * SUF), bf16),
        ),
        in_specs=[pl.BlockSpec(memory_space=pltpu.SMEM)] * len(scalars) + [vmem] * len(arrays),
        out_specs=[vmem] * 2,
        scratch_shapes=[
            pltpu.VMEM((8, 2, HD, kv_own.shape[2]), bf16),
            pltpu.VMEM((16, rows, width), bf16),
            pltpu.VMEM((8, 2, 192, 192), bf16),
            pltpu.VMEM((4, 2, 4, 2, 2, HD, 192), bf16),
            pltpu.VMEM((4, 2, 2, 3, 192, 256), bf16),
            pltpu.VMEM((192, 192), bf16),
            pltpu.VMEM((4, SUF, HD), bf16),
            pltpu.VMEM((4, HD, SUF), bf16),
            pltpu.VMEM((4, HD, SUF), bf16),
            pltpu.VMEM((4, HD, SUF), bf16),
            pltpu.VMEM((16, HD, 128), bf16),
            pltpu.VMEM((4, 2, rows, width), bf16),
            pltpu.VMEM((4, 2, rows, width), bf16),
            pltpu.VMEM((4, rows, width), bf16),
            pltpu.VMEM((4, rows, width), f32),
            pltpu.VMEM((2, 64, width), bf16),
            pltpu.VMEM((4, 64, width), bf16),
            pltpu.VMEM((4, 64, width), bf16),
            pltpu.VMEM((rows, width), bf16),
            pltpu.SemaphoreType.DMA((SEMS,)),
            pltpu.SemaphoreType.DMA((SEMS,)),
            pltpu.SemaphoreType.DMA((16,)),
            pltpu.SemaphoreType.DMA((16,)),
            pltpu.SemaphoreType.DMA((8,)),
        ],
        compiler_params=pltpu.CompilerParams(
            collective_id=0, has_side_effects=True, vmem_limit_bytes=67_043_328
        ),
        name="layer_kernel",
    )(*scalars, *arrays)


def local(
    tokens,
    attention_gain,
    feed_gain,
    w_query,
    w_key,
    w_value,
    w_out,
    w_gate,
    w_up,
    w_down,
    prefix_cache,
    lengths,
    member,
    owners,
):
    req, mdl = places()
    prefix_length = prefix_cache.shape[2]
    half = np.arange(HD // 2).astype(np.float32)
    frequency = np.float32(rope_base) ** (-(half * np.float32(2.0) / np.float32(HD)))
    positions = (np.arange(SUF) + prefix_length).astype(np.float32)
    angles = (frequency[:, None] * positions[None, :]).astype(np.float64)
    hidden, cache = layer(
        (lengths, member, owners),
        (
            prefix_cache[:, 0].transpose(0, 2, 1),
            tokens,
            w_query,
            w_key.T,
            w_value.T,
            w_out,
            w_gate,
            w_up,
            w_down.T,
            attention_gain[None, :],
            feed_gain[None, :],
            np.cos(angles).astype(np.float32),
            np.sin(angles).astype(np.float32),
        ),
    )
    own_offset = (mdl % 4) * tokens.shape[0] + jnp.arange(tokens.shape[0], dtype=jnp.int32)
    own_length = lax.dynamic_index_in_dim(lengths, req * 4 + mdl // 4, keepdims=False)
    own_valid = own_offset < own_length
    hidden = (hidden.astype(jnp.float32) * own_valid[:, None].astype(jnp.float32)).astype(
        jnp.bfloat16
    )
    return (hidden, cache.transpose(0, 2, 1))


def solution(mesh):
    placed = (
        P(("req", "mdl"), None),
        P(),
        P(),
        P("req", "mdl"),
        P("req", "mdl"),
        P("req", "mdl"),
        P("mdl", "req"),
        P("req", "mdl"),
        P("req", "mdl"),
        P("mdl", "req"),
        P(None, "req", None, "mdl"),
        P(),
        P(),
        P(),
    )
    return jax.shard_map(
        local,
        mesh=mesh,
        in_specs=placed,
        out_specs=(P(("req", "mdl"), None), P(None, "req", "mdl")),
        check_vma=False,
    )
```

time: 181 us -> 156 us (0.86)
  Pallas kernels: 174 us -> 147 us
  local copies, waits for them, and re-layouts: 2.48 us -> 4.54 us
    pallas_call x3 -> x1, Pallas kernels: 174 us -> 147 us  [layer(): pl.pallas_call(layer_kernel, out_shape=(jax.ShapeDtypeStruct((rows, width...]
    unnamed x4 -> x11, local copies, waits for them, and re-layouts: 0.01 us -> 2.77 us
where the time goes in v3:
time: 156 us
  Pallas kernels  147 us (94%)
  local copies, waits for them, and re-layouts  4.54 us (3%)
  other arithmetic  3.08 us (2%)
    pallas_call x1, Pallas kernels, layer(): pl.pallas_call(layer_kernel, out_shape=(jax.ShapeDtypeStruct((rows, width...  147 us

profile of v3, /device:TPU:1, one launch (start us, length us, event | category | flops | bytes accessed | tf_op | source)
XLA Modules:
  0.0 155.5 jit_solution(3693321363581624754)
XLA Ops:
  0.7 0.0 copy-start.4
  0.7 0.6 copy-done.4
  1.3 0.6 dynamic_slice.4
  1.9 1.2 compare_convert_fusion
  3.0 0.0 copy-start.1
  3.1 0.7 copy-done.1
  3.7 0.0 copy-start.2
  3.7 0.6 broadcast_in_dim.7.gain_ref
  4.3 0.1 copy-done.2
  4.4 0.6 broadcast_in_dim.8.feed_gain_ref
  5.0 147.2 %layer_kernel.1 = (bf16[128,1536]{1,0:T(8,128)(2,1)}, bf16[2,48,2048]{2,1,0:T(8,128)(2,1)}) custom-call(s32[32]{0:T(128)} %lengths.1, s32[32]{0:T(128)} %member.1, s32[8]{0:T(128)} %owners.1, bf16[2,48,4096]{2,1,0:T(8,128)(2,1)} %bitcast.8, bf16[128,1536]{1,0:T(8,128)(2,1)} %tok_in.1, bf16[192,96]{1,0:T(8,128)(2,1)} %wq_in.1, bf16[48,192]{1,0:T(8,128)(2,1)} %bitcast.11, ...), custom_call_target="tpu_custom_call" | custom-call | tf_op jit(solution)/shard_map/layer_kernel/pallas_call | solution.py:553
  152.3 0.0 copy-start.3
  152.3 0.6 copy-done.3
  152.9 0.0 copy-start
  152.9 1.9 %multiply_convert_fusion = bf16[128,1536]{1,0:T(8,128)(2,1)} fusion(bf16[128,1536]{1,0:T(8,128)(2,1)} %get-tuple-element.4, f32[128]{0:T(128)S(1)} %copy-done.3), kind=kLoop, calls=%fused_computation | loop fusion | flops 589824 | bytes 786944 | tf_op jit(solution)/shard_map/convert_element_type | solution.py:637
  154.8 0.0 copy-done
  154.8 0.7 copy.19
Async XLA Ops:
  0.7 0.7 copy-start.4
  3.0 0.7 copy-start.1
  3.7 0.7 copy-start.2
  152.3 0.6 copy-start.3
  152.9 1.9 %copy-start = (bf16[2,48,2048]{2,1,0:T(8,128)(2,1)S(1)}, bf16[2,48,2048]{2,1,0:T(8,128)(2,1)}, u32[]{:S(2)}) copy-start(bf16[2,48,2048]{2,1,0:T(8,128)(2,1)} %get-tuple-element.5) | copy-start | bytes 1179652

commit v4 on v3

--- a/solution.py
+++ b/solution.py
@@ -67,11 +67,17 @@
         self.up = self.hub.copy(src, block, self.dev(self.up_to))
         self.down = self.hub.copy(src, block, self.dev(self.down_to))
 
-    def arrive(self):
+    def near(self):
         self.up.wait_recv()
+        self.down.wait_recv()
+
+    def arrive(self, waited=False):
+        if not waited:
+            self.up.wait_recv()
         low = self.piece(self.down_to, 0)
         self.far_low = self.hub.copy(low, low, self.dev(self.up_to))
-        self.down.wait_recv()
+        if not waited:
+            self.down.wait_recv()
         high = self.piece(self.up_to, 1)
         self.far_high = self.hub.copy(high, high, self.dev(self.down_to))
 
@@ -79,9 +85,37 @@
         self.far_low.wait_recv()
         self.far_high.wait_recv()
 
+    def start_split(self, src):
+        here, up, down = self.here, self.dev(self.up_to), self.dev(self.down_to)
+        self.up = self.hub.copy(src.at[0], self.piece(here, 0), up)
+        self.down = self.hub.copy(src.at[1], self.piece(here, 1), down)
+        self.up_rest = self.hub.copy(src.at[1], self.piece(here, 1), up)
+        self.down_rest = self.hub.copy(src.at[0], self.piece(here, 0), down)
+
+    def rest(self):
+        self.up_rest.wait_recv()
+        self.down_rest.wait_recv()
+
     def share(self, u, device):
         block = self.region(u)
         return self.hub.copy(block, block, device, awaited=False)
+
+
+class Direct:
+    def __init__(self, hub, region, dev, u):
+        self.hub, self.region, self.dev, self.here = hub, region, dev, u
+
+    def start(self, src=None):
+        block = self.region(self.here)
+        src = block if src is None else src
+        self.sent = [
+            self.hub.copy(src, block, self.dev(lax.rem(self.here + step, 4)))
+            for step in (1, 3, 2)
+        ]
+
+    def finish(self):
+        for made in self.sent:
+            made.wait_recv()
 
 
 class Spread:
@@ -134,7 +168,8 @@
             made.wait_recv()
 
 
-SEMS = 116
+SEMS = 130
+KV_EARLY = 3072
 
 
 def layer_kernel(
@@ -172,7 +207,7 @@
 
     barrier = pltpu.get_barrier_semaphore()
     peers = [kv_dev(x, 1 - yh)]
-    peers += [x_dev(lax.rem(x + step, 4)) for step in (1, 3)]
+    peers += [x_dev(lax.rem(x + step, 4)) for step in (1, 2, 3)]
     peers += [y_dev(lax.rem(y + step, 4)) for step in (1, 3)]
     peers += [{"req": req, "mdl": lax.rem(mdl + step, 16)} for step in range(1, 16)]
     for peer in peers:
@@ -196,12 +231,33 @@
     pl.semaphore_wait(barrier, len(peers))
 
     hub = Hub(send, recv)
-    kv = Spread(
-        hub, kv_in,
-        lambda u, v: kv_all.at[u * 2 + v, :, rows, :],
-        lambda ref, h: ref.at[h],
-        x, yh, kv_dev, partner,
-    )
+    early, late = pl.ds(0, KV_EARLY), pl.ds(KV_EARLY, kv_all.shape[3] - KV_EARLY)
+    kv_ring = Ring(
+        hub,
+        lambda u: kv_all.at[u * 2 + yh, :, rows],
+        lambda u, h: kv_all.at[u * 2 + yh, h, rows],
+        x_dev, x,
+    )
+    kv_other = Ring(
+        hub,
+        lambda u: kv_all.at[u * 2 + 1 - yh, :, rows, early],
+        lambda u, h: kv_all.at[u * 2 + 1 - yh, h, rows, early],
+        x_dev, x,
+    )
+    kv_pair = kv_dev(x, 1 - yh)
+    handed = []
+
+    def hand(block):
+        handed.append(hub.copy(block, block, partner))
+
+    def cross(u):
+        block = kv_all.at[u * 2 + yh, :, rows, late]
+        return hub.copy(block, block, kv_pair)
+
+    def crossed(u, made):
+        made.wait_recv()
+        hand(kv_all.at[u * 2 + 1 - yh, :, rows, late])
+
     tok = Spread(
         hub, tok_in,
         lambda u, v: tok_all.at[u * 4 + v * 2 + core],
@@ -214,18 +270,8 @@
         lambda ref, h: ref.at[pl.ds(96 * h, 96)],
         x, yh, kv_dev, partner,
     )
-    wo_x = Ring(
-        hub,
-        lambda u: wo.at[z, core, u, yh, yl],
-        lambda u, h: wo.at[z, core, u, yh, yl, pl.ds(48 * h, 48)],
-        x_dev, x,
-    )
-    wo_y = Ring(
-        hub,
-        lambda u: wo.at[z, core, :, u // 2, lax.rem(u, 2)],
-        lambda u, h: wo.at[z, core, pl.ds(2 * h, 2), u // 2, lax.rem(u, 2)],
-        y_dev, y,
-    )
+    wo_x = Direct(hub, lambda u: wo.at[z, core, u, yh, yl], x_dev, x)
+    wo_y = Direct(hub, lambda u: wo.at[z, core, :, u // 2, lax.rem(u, 2)], y_dev, y)
     wo_z = Ring(
         hub,
         lambda u: wo.at[u, core],
@@ -340,61 +386,82 @@
 
         return carry
 
+    kv_here = kv_ring.region(x)
     wo_x.start(wo_in)
+    tok.start_pair()
+    kv_ring.start_split(kv_in)
+    tok.start_ring()
+    qkv.start_pair()
+    kv_over = hub.copy(kv_in, kv_here, kv_pair)
     qkv.start_ring()
-    qkv.start_pair()
-    tok.start_pair()
-    tok.start_ring()
+    handed.append(hub.copy(kv_in, kv_here, partner))
     store(pack, wqkv.at[req, core])
-    wo_x.arrive()
-    qkv.ring_arrived(0)
+    keep[0].wait()
+    wo_x.finish()
+    wo_y.start()
+    kv_ring.arrive()
+    tok.pair_arrived()
+    tok.ring_arrived(0)
     qkv.pair_arrived()
-    kv.start_ring()
-    wo_x.finish()
-    keep[0].wait()
-    wo_y.start()
-    kv.start_pair()
     for made in keep[1:4]:
         made.wait()
     wm_x.start()
+    kv_ring.rest()
+    cross_low = cross(kv_ring.down_to)
+    cross_high = cross(kv_ring.up_to)
+    hand(kv_ring.region(kv_ring.down_to))
+    hand(kv_ring.region(kv_ring.up_to))
+    qkv.ring_arrived(0)
+    kv_over.wait_recv()
+    kv_other.start_split(kv_other.region(x))
+    hand(kv_all.at[x * 2 + 1 - yh, :, rows])
+    tok.ring_arrived(1)
+    qkv.ring_arrived(1)
+    kv_ring.finish()
+    cross_far = cross(kv_ring.opposite)
+    hand(kv_ring.region(kv_ring.opposite))
     wm_y[0].start()
-    tok.pair_arrived()
-    tok.ring_arrived(0)
-    qkv.far_arrived(0)
-    wo_y.arrive()
-    tok.ring_arrived(1)
-    kv.ring_arrived(0)
-    tok.far_arrived(0)
-    tok.far_arrived(1)
-    wm_x.arrive()
-    wm_y[3].start()
-    wm_y[1].start()
-    kv.pair_arrived()
-    qkv.ring_arrived(1)
     wo_y.finish()
     wo_z.start()
     wo_z.share(z, partner)
+    wm_x.near()
+    wm_y[3].start()
+    wm_y[1].start()
+    tok.far_arrived(0)
+    tok.far_arrived(1)
+    qkv.far_arrived(0)
+    kv_other.arrive()
+    wm_x.arrive(True)
     qkv.far_arrived(1)
-    wm_y[0].arrive()
     for made in keep[4:]:
         made.wait()
     tok.shared()
     qkv.shared()
     lax.fori_loop(0, 4, project, 0)
-    kv.far_arrived(0)
+    crossed(kv_ring.down_to, cross_low)
+    crossed(kv_ring.up_to, cross_high)
+    kv_other.rest()
+    hand(kv_other.region(kv_other.down_to))
+    hand(kv_other.region(kv_other.up_to))
+    crossed(kv_ring.opposite, cross_far)
+    wm_y[0].arrive()
     wo_z.arrive()
     wo_z.share(wo_z.down_to, partner)
     wo_z.share(wo_z.up_to, partner)
+    kv_other.finish()
+    hand(kv_other.region(kv_other.opposite))
+    for made in handed:
+        made.wait_recv()
+    attend(0, 0)
+    wm_x.finish()
+    wm_y[2].start()
+    attend(1, 0)
+    wo_z.finish()
+    wo_z.share(wo_z.opposite, partner)
     wm_y[3].arrive()
     wm_y[1].arrive()
-    kv.ring_arrived(1)
-    wm_x.finish()
-    wm_y[2].start()
-    wo_z.finish()
-    wo_z.share(wo_z.opposite, partner)
-    kv.far_arrived(1)
-    kv.shared()
-    lax.fori_loop(0, 4, attend, 0)
+    attend(2, 0)
+    attend(3, 0)
     wm_y[2].arrive()
     att[mdl] = att_out[z, :, pl.ds(pl.multiple_of(quarter * 128, 128), 128)]
 

time: 156 us -> 148 us (0.949)
  Pallas kernels: 147 us -> 139 us
    pallas_call x1, Pallas kernels: 147 us -> 139 us  [layer(): pl.pallas_call(layer_kernel, out_shape=(jax.ShapeDtypeStruct((rows, width...]
where the time goes in v4:
time: 148 us
  Pallas kernels  139 us (94%)
  local copies, waits for them, and re-layouts  4.54 us (3%)
  other arithmetic  3.08 us (2%)
    pallas_call x1, Pallas kernels, layer(): pl.pallas_call(layer_kernel, out_shape=(jax.ShapeDtypeStruct((rows, width...  139 us

profile of v4, /device:TPU:1, one launch (start us, length us, event | category | flops | bytes accessed | tf_op | source)
XLA Modules:
  0.0 147.6 jit_solution(11736406302922977799)
XLA Ops:
  0.7 0.0 copy-start.4
  0.7 0.6 copy-done.4
  1.3 0.6 dynamic_slice.4
  1.9 1.2 compare_convert_fusion
  3.0 0.0 copy-start.1
  3.1 0.7 copy-done.1
  3.7 0.0 copy-start.2
  3.7 0.6 broadcast_in_dim.7.gain_ref
  4.3 0.1 copy-done.2
  4.4 0.6 broadcast_in_dim.8.feed_gain_ref
  5.0 139.3 %layer_kernel.1 = (bf16[128,1536]{1,0:T(8,128)(2,1)}, bf16[2,48,2048]{2,1,0:T(8,128)(2,1)}) custom-call(s32[32]{0:T(128)} %lengths.1, s32[32]{0:T(128)} %member.1, s32[8]{0:T(128)} %owners.1, bf16[2,48,4096]{2,1,0:T(8,128)(2,1)} %bitcast.8, bf16[128,1536]{1,0:T(8,128)(2,1)} %tok_in.1, bf16[192,96]{1,0:T(8,128)(2,1)} %wq_in.1, bf16[48,192]{1,0:T(8,128)(2,1)} %bitcast.11, ...), custom_call_target="tpu_custom_call" | custom-call | tf_op jit(solution)/shard_map/layer_kernel/pallas_call | solution.py:620
  144.4 0.0 copy-start.3
  144.4 0.6 copy-done.3
  144.9 0.0 copy-start
  144.9 1.9 %multiply_convert_fusion = bf16[128,1536]{1,0:T(8,128)(2,1)} fusion(bf16[128,1536]{1,0:T(8,128)(2,1)} %get-tuple-element.4, f32[128]{0:T(128)S(1)} %copy-done.3), kind=kLoop, calls=%fused_computation | loop fusion | flops 589824 | bytes 786944 | tf_op jit(solution)/shard_map/convert_element_type | solution.py:704
  146.9 0.0 copy-done
  146.9 0.7 copy.19
Async XLA Ops:
  0.7 0.7 copy-start.4
  3.0 0.7 copy-start.1
  3.7 0.7 copy-start.2
  144.4 0.6 copy-start.3
  144.9 1.9 %copy-start = (bf16[2,48,2048]{2,1,0:T(8,128)(2,1)S(1)}, bf16[2,48,2048]{2,1,0:T(8,128)(2,1)}, u32[]{:S(2)}) copy-start(bf16[2,48,2048]{2,1,0:T(8,128)(2,1)} %get-tuple-element.5) | copy-start | bytes 1179652

commit v5 on v4

--- a/solution.py
+++ b/solution.py
@@ -85,20 +85,22 @@
         self.far_low.wait_recv()
         self.far_high.wait_recv()
 
-    def start_split(self, src):
-        here, up, down = self.here, self.dev(self.up_to), self.dev(self.down_to)
-        self.up = self.hub.copy(src.at[0], self.piece(here, 0), up)
-        self.down = self.hub.copy(src.at[1], self.piece(here, 1), down)
-        self.up_rest = self.hub.copy(src.at[1], self.piece(here, 1), up)
-        self.down_rest = self.hub.copy(src.at[0], self.piece(here, 0), down)
+    def start_split(self, src=None):
+        up, down = self.dev(self.up_to), self.dev(self.down_to)
+        to = [self.piece(self.here, h) for h in range(2)]
+        of = to if src is None else [src.at[h] for h in range(2)]
+        self.up = self.hub.copy(of[0], to[0], up)
+        self.down = self.hub.copy(of[1], to[1], down)
+        self.up_rest = self.hub.copy(of[1], to[1], up)
+        self.down_rest = self.hub.copy(of[0], to[0], down)
 
     def rest(self):
         self.up_rest.wait_recv()
         self.down_rest.wait_recv()
 
-    def share(self, u, device):
+    def share(self, u, device, awaited=True):
         block = self.region(u)
-        return self.hub.copy(block, block, device, awaited=False)
+        return self.hub.copy(block, block, device, awaited)
 
 
 class Direct:
@@ -168,7 +170,7 @@
             made.wait_recv()
 
 
-SEMS = 130
+SEMS = 136
 KV_EARLY = 3072
 
 
@@ -280,8 +282,8 @@
     )
     wm_x = Ring(
         hub,
-        lambda u: wm.at[u, yh, yl],
-        lambda u, h: wm.at[u, yh, yl, :, pl.ds(96 * h, 96)],
+        lambda u: wm.at[u, yh, yl, 0:2],
+        lambda u, h: wm.at[u, yh, yl, 0:2, pl.ds(96 * h, 96)],
         x_dev, x,
     )
 
@@ -289,12 +291,24 @@
         u_x = lax.rem(x + step, 4)
         return Ring(
             hub,
-            lambda u: wm.at[u_x, u // 2, lax.rem(u, 2)],
-            lambda u, h: wm.at[u_x, u // 2, lax.rem(u, 2), :, pl.ds(96 * h, 96)],
+            lambda u: wm.at[u_x, u // 2, lax.rem(u, 2), 0:2],
+            lambda u, h: wm.at[u_x, u // 2, lax.rem(u, 2), 0:2, pl.ds(96 * h, 96)],
             y_dev, y,
         )
 
     wm_y = [wm_ring(step) for step in range(4)]
+    wd_y = Ring(
+        hub,
+        lambda u: wm.at[x, u // 2, lax.rem(u, 2), 2],
+        lambda u, h: wm.at[x, u // 2, lax.rem(u, 2), 2, pl.ds(96 * h, 96)],
+        y_dev, y,
+    )
+    wd_x = Ring(
+        hub,
+        lambda u: wm.at[u, :, :, 2],
+        lambda u, h: wm.at[u, h, :, 2],
+        x_dev, x,
+    )
 
     def project(r, carry):
         numbers = tok_all[pl.ds(4 * r, 4)].reshape(SUF, width).astype(jnp.float32)
@@ -399,6 +413,7 @@
     keep[0].wait()
     wo_x.finish()
     wo_y.start()
+    wd_y.start(wd_in)
     kv_ring.arrive()
     tok.pair_arrived()
     tok.ring_arrived(0)
@@ -413,7 +428,7 @@
     hand(kv_ring.region(kv_ring.up_to))
     qkv.ring_arrived(0)
     kv_over.wait_recv()
-    kv_other.start_split(kv_other.region(x))
+    kv_other.start_split()
     hand(kv_all.at[x * 2 + 1 - yh, :, rows])
     tok.ring_arrived(1)
     qkv.ring_arrived(1)
@@ -423,7 +438,8 @@
     wm_y[0].start()
     wo_y.finish()
     wo_z.start()
-    wo_z.share(z, partner)
+    wo_z.share(z, partner, False)
+    wd_y.arrive()
     wm_x.near()
     wm_y[3].start()
     wm_y[1].start()
@@ -432,6 +448,8 @@
     qkv.far_arrived(0)
     kv_other.arrive()
     wm_x.arrive(True)
+    wd_y.finish()
+    wd_x.start()
     qkv.far_arrived(1)
     for made in keep[4:]:
         made.wait()
@@ -444,20 +462,21 @@
     hand(kv_other.region(kv_other.down_to))
     hand(kv_other.region(kv_other.up_to))
     crossed(kv_ring.opposite, cross_far)
-    wm_y[0].arrive()
-    wo_z.arrive()
-    wo_z.share(wo_z.down_to, partner)
-    wo_z.share(wo_z.up_to, partner)
     kv_other.finish()
     hand(kv_other.region(kv_other.opposite))
     for made in handed:
         made.wait_recv()
+    wm_y[0].arrive()
+    wo_z.arrive()
+    wo_z.share(wo_z.down_to, partner, False)
+    wo_z.share(wo_z.up_to, partner, False)
     attend(0, 0)
     wm_x.finish()
     wm_y[2].start()
+    wd_x.arrive()
     attend(1, 0)
     wo_z.finish()
-    wo_z.share(wo_z.opposite, partner)
+    wo_z.share(wo_z.opposite, partner, False)
     wm_y[3].arrive()
     wm_y[1].arrive()
     attend(2, 0)
@@ -505,17 +524,22 @@
             axis=1,
         )
         here = slice(384 * u, 384 * u + 384)
-        own_rows[:, here] = (tok_in[:, here].astype(jnp.float32) + attention).astype(jnp.bfloat16)
+        own_rows[:, here] = (tok_all[mdl, :, here].astype(jnp.float32) + attention).astype(jnp.bfloat16)
 
     def peer(du, flip=False):
         other = 1 - core if flip else core
         return {"req": req, "mdl": lax.rem(z + du, 4) * 4 + yl * 2 + other}
 
     go = hub.copy
-    up = go(own_rows, own_rows, peer(1))
-    down = go(own_rows, own_rows, peer(3))
-    across = go(own_rows, own_rows, peer(0, True))
-    for ring in wm_y:
+    gathered = Ring(
+        hub,
+        lambda u: rows_all.at[u, core],
+        lambda u, h: rows_all.at[u, core, pl.ds(64 * h, 64)],
+        z_dev, z,
+    )
+    gathered.start_split()
+    across = go(own_rows, own_rows, partner)
+    for ring in wm_y + [wd_x]:
         ring.finish()
 
     def feed(slot, du):
@@ -557,36 +581,29 @@
 
     across.wait_recv()
     pair0 = feed(0, 0)
-    up.wait_recv()
-    low = rows_all.at[lax.rem(z + 3, 4), core]
-    far_a = go(low.at[pl.ds(0, 64)], low.at[pl.ds(0, 64)], peer(1))
-    low_p = go(low, low, peer(0, True))
-    down.wait_recv()
-    high = rows_all.at[lax.rem(z + 1, 4), core]
-    far_b = go(high.at[pl.ds(64, 64)], high.at[pl.ds(64, 64)], peer(3))
-    high_p = go(high, high, peer(0, True))
+    gathered.arrive()
+    gathered.up_rest.wait_recv()
+    low_p = gathered.share(gathered.down_to, partner)
+    gathered.down_rest.wait_recv()
+    high_p = gathered.share(gathered.up_to, partner)
     low_p.wait_recv()
     pair3 = feed(3, 3)
-    high_p.wait_recv()
-    pair1 = feed(1, 1)
-    far = rows_all.at[lax.rem(z + 2, 4), core]
-    far_a.wait_recv()
-    far_pa = go(far.at[pl.ds(0, 64)], far.at[pl.ds(0, 64)], peer(0, True))
-    far_b.wait_recv()
-    far_pb = go(far.at[pl.ds(64, 64)], far.at[pl.ds(64, 64)], peer(0, True))
+    gathered.finish()
+    far_p = gathered.share(gathered.opposite, partner)
     pair_sum(3, pair3)
     plain[0] = sums[3, 0:64].astype(jnp.bfloat16)
     plain_a = go(plain.at[0], plain.at[2], peer(3))
-    pair_sum(1, pair1)
-    plain[1] = sums[1, 64:128].astype(jnp.bfloat16)
-    plain_b = go(plain.at[1], plain.at[3], peer(1))
-    far_pa.wait_recv()
-    far_pb.wait_recv()
+    far_p.wait_recv()
     pair2 = feed(2, 2)
+    high_p.wait_recv()
     pair_sum(2, pair2)
     to_relay[...] = sums[2].astype(jnp.bfloat16)
     relay_a = go(to_relay.at[pl.ds(0, 64)], relay.at[0], peer(1))
     relay_b = go(to_relay.at[pl.ds(64, 64)], relay.at[1], peer(3))
+    pair1 = feed(1, 1)
+    pair_sum(1, pair1)
+    plain[1] = sums[1, 64:128].astype(jnp.bfloat16)
+    plain_b = go(plain.at[1], plain.at[3], peer(1))
     pair_sum(0, pair0)
     relay_a.wait_recv()
     joined[0] = (sums[1, 0:64] + relay[0].astype(jnp.float32)).astype(jnp.bfloat16)
@@ -605,7 +622,11 @@
             + plain[2 + h].astype(jnp.float32)
             + joined[2 + h].astype(jnp.float32)
         )
-        out_ref[here, :] = (own_rows[here, :].astype(jnp.float32) + feed_sum).astype(jnp.bfloat16)
+        place = quarter * 128 + 64 * h + lax.broadcasted_iota(jnp.int32, (64, 1), 0)
+        live = (place < lengths[req * 4 + z]).astype(jnp.float32)
+        out_ref[here, :] = (
+            (own_rows[here, :].astype(jnp.float32) + feed_sum) * live
+        ).astype(jnp.bfloat16)
     for i in range(4):
         for j in range(4):
             exchange(i, j, True)
@@ -617,13 +638,15 @@
     rows, width = tokens.shape
     bf16, f32 = jnp.bfloat16, jnp.float32
     vmem = pl.BlockSpec(memory_space=pltpu.VMEM)
+    hbm = pl.BlockSpec(memory_space=pl.ANY)
     return pl.pallas_call(
         layer_kernel,
         out_shape=(
             jax.ShapeDtypeStruct((rows, width), bf16),
             jax.ShapeDtypeStruct((2, HALF, 4 * SUF), bf16),
         ),
-        in_specs=[pl.BlockSpec(memory_space=pltpu.SMEM)] * len(scalars) + [vmem] * len(arrays),
+        in_specs=[pl.BlockSpec(memory_space=pltpu.SMEM)] * len(scalars)
+        + [hbm, hbm, vmem, vmem, vmem, hbm, hbm, hbm, hbm, vmem, vmem, vmem, vmem],
         out_specs=[vmem] * 2,
         scratch_shapes=[
             pltpu.VMEM((8, 2, HD, kv_own.shape[2]), bf16),
@@ -674,7 +697,6 @@
     member,
     owners,
 ):
-    req, mdl = places()
     prefix_length = prefix_cache.shape[2]
     half = np.arange(HD // 2).astype(np.float32)
     frequency = np.float32(rope_base) ** (-(half * np.float32(2.0) / np.float32(HD)))
@@ -698,12 +720,6 @@
             np.sin(angles).astype(np.float32),
         ),
     )
-    own_offset = (mdl % 4) * tokens.shape[0] + jnp.arange(tokens.shape[0], dtype=jnp.int32)
-    own_length = lax.dynamic_index_in_dim(lengths, req * 4 + mdl // 4, keepdims=False)
-    own_valid = own_offset < own_length
-    hidden = (hidden.astype(jnp.float32) * own_valid[:, None].astype(jnp.float32)).astype(
-        jnp.bfloat16
-    )
     return (hidden, cache.transpose(0, 2, 1))
 
 

time: 148 us -> 147 us (level)
  other arithmetic: 3.08 us -> 0 us
  Pallas kernels: 139 us -> 141 us
    convert_element_type x2 -> x0, other arithmetic: 3.08 us -> none  [the longest x1 1.92 us: local(): (hidden.astype(jnp.float32) * own_valid[:, None].astype(jnp.float32)).ast...]
    pallas_call x1, Pallas kernels: 139 us -> 141 us  [layer(): pl.pallas_call(layer_kernel, out_shape=(jax.ShapeDtypeStruct((rows, width...]
    unnamed x11 -> x8, local copies, waits for them, and re-layouts: 2.77 us -> 3.34 us
where the time goes in v5:
time: 147 us; the launch traced here: 146 us
  Pallas kernels  141 us (96%)
  local copies, waits for them, and re-layouts  4.53 us (3%)
    pallas_call x1, Pallas kernels, layer(): pl.pallas_call(layer_kernel, out_shape=(jax.ShapeDtypeStruct((rows, width...  141 us
    unnamed x8, local copies, waits for them, and re-layouts  3.34 us

profile of v5, /device:TPU:1, one launch (start us, length us, event | category | flops | bytes accessed | tf_op | source)
XLA Modules:
  0.0 146.3 jit_solution(6024947214551987239)
XLA Ops:
  0.6 0.0 copy-start.1
  0.6 0.7 copy-done.1
  1.3 0.0 copy-start.2
  1.3 0.6 broadcast_in_dim.6.gain_ref
  1.9 0.1 copy-done.2
  2.0 0.6 broadcast_in_dim.7.feed_gain_ref
  2.6 141.1 %layer_kernel.1 = (bf16[128,1536]{1,0:T(8,128)(2,1)}, bf16[2,48,2048]{2,1,0:T(8,128)(2,1)}) custom-call(s32[32]{0:T(128)} %lengths.1, s32[32]{0:T(128)} %member.1, s32[8]{0:T(128)} %owners.1, bf16[2,48,4096]{2,1,0:T(8,128)(2,1)} %bitcast.7, bf16[128,1536]{1,0:T(8,128)(2,1)} %tok_in.1, bf16[192,96]{1,0:T(8,128)(2,1)} %wq_in.1, bf16[48,192]{1,0:T(8,128)(2,1)} %bitcast.10, ...), custom_call_target="tpu_custom_call" | custom-call | tf_op jit(solution)/shard_map/layer_kernel/pallas_call | solution.py:642
  143.7 0.0 copy-start
  143.8 1.8 %copy.20 = bf16[128,1536]{1,0:T(8,128)(2,1)} copy(bf16[128,1536]{1,0:T(8,128)(2,1)} %get-tuple-element.8) | data formatting | bytes 786432
  145.6 0.0 copy-done
  145.6 0.7 copy.21
Async XLA Ops:
  0.6 0.7 copy-start.1
  1.3 0.7 copy-start.2
  143.7 1.8 %copy-start = (bf16[2,48,2048]{2,1,0:T(8,128)(2,1)S(1)}, bf16[2,48,2048]{2,1,0:T(8,128)(2,1)}, u32[]{:S(2)}) copy-start(bf16[2,48,2048]{2,1,0:T(8,128)(2,1)} %get-tuple-element.5) | copy-start | bytes 1179652

commit v6 on v5

--- a/solution.py
+++ b/solution.py
@@ -282,8 +282,8 @@
     )
     wm_x = Ring(
         hub,
-        lambda u: wm.at[u, yh, yl, 0:2],
-        lambda u, h: wm.at[u, yh, yl, 0:2, pl.ds(96 * h, 96)],
+        lambda u: wm.at[u, yh, yl],
+        lambda u, h: wm.at[u, yh, yl, :, pl.ds(96 * h, 96)],
         x_dev, x,
     )
 
@@ -291,24 +291,12 @@
         u_x = lax.rem(x + step, 4)
         return Ring(
             hub,
-            lambda u: wm.at[u_x, u // 2, lax.rem(u, 2), 0:2],
-            lambda u, h: wm.at[u_x, u // 2, lax.rem(u, 2), 0:2, pl.ds(96 * h, 96)],
+            lambda u: wm.at[u_x, u // 2, lax.rem(u, 2)],
+            lambda u, h: wm.at[u_x, u // 2, lax.rem(u, 2), :, pl.ds(96 * h, 96)],
             y_dev, y,
         )
 
     wm_y = [wm_ring(step) for step in range(4)]
-    wd_y = Ring(
-        hub,
-        lambda u: wm.at[x, u // 2, lax.rem(u, 2), 2],
-        lambda u, h: wm.at[x, u // 2, lax.rem(u, 2), 2, pl.ds(96 * h, 96)],
-        y_dev, y,
-    )
-    wd_x = Ring(
-        hub,
-        lambda u: wm.at[u, :, :, 2],
-        lambda u, h: wm.at[u, h, :, 2],
-        x_dev, x,
-    )
 
     def project(r, carry):
         numbers = tok_all[pl.ds(4 * r, 4)].reshape(SUF, width).astype(jnp.float32)
@@ -413,7 +401,6 @@
     keep[0].wait()
     wo_x.finish()
     wo_y.start()
-    wd_y.start(wd_in)
     kv_ring.arrive()
     tok.pair_arrived()
     tok.ring_arrived(0)
@@ -439,7 +426,6 @@
     wo_y.finish()
     wo_z.start()
     wo_z.share(z, partner, False)
-    wd_y.arrive()
     wm_x.near()
     wm_y[3].start()
     wm_y[1].start()
@@ -448,8 +434,6 @@
     qkv.far_arrived(0)
     kv_other.arrive()
     wm_x.arrive(True)
-    wd_y.finish()
-    wd_x.start()
     qkv.far_arrived(1)
     for made in keep[4:]:
         made.wait()
@@ -473,7 +457,6 @@
     attend(0, 0)
     wm_x.finish()
     wm_y[2].start()
-    wd_x.arrive()
     attend(1, 0)
     wo_z.finish()
     wo_z.share(wo_z.opposite, partner, False)
@@ -539,7 +522,7 @@
     )
     gathered.start_split()
     across = go(own_rows, own_rows, partner)
-    for ring in wm_y + [wd_x]:
+    for ring in wm_y:
         ring.finish()
 
     def feed(slot, du):
@@ -590,20 +573,20 @@
     pair3 = feed(3, 3)
     gathered.finish()
     far_p = gathered.share(gathered.opposite, partner)
+    high_p.wait_recv()
+    pair1 = feed(1, 1)
     pair_sum(3, pair3)
     plain[0] = sums[3, 0:64].astype(jnp.bfloat16)
     plain_a = go(plain.at[0], plain.at[2], peer(3))
     far_p.wait_recv()
     pair2 = feed(2, 2)
-    high_p.wait_recv()
+    pair_sum(1, pair1)
+    plain[1] = sums[1, 64:128].astype(jnp.bfloat16)
+    plain_b = go(plain.at[1], plain.at[3], peer(1))
     pair_sum(2, pair2)
     to_relay[...] = sums[2].astype(jnp.bfloat16)
     relay_a = go(to_relay.at[pl.ds(0, 64)], relay.at[0], peer(1))
     relay_b = go(to_relay.at[pl.ds(64, 64)], relay.at[1], peer(3))
-    pair1 = feed(1, 1)
-    pair_sum(1, pair1)
-    plain[1] = sums[1, 64:128].astype(jnp.bfloat16)
-    plain_b = go(plain.at[1], plain.at[3], peer(1))
     pair_sum(0, pair0)
     relay_a.wait_recv()
     joined[0] = (sums[1, 0:64] + relay[0].astype(jnp.float32)).astype(jnp.bfloat16)

time: 147 us -> 144 us (0.980)
  Pallas kernels: 141 us -> 138 us
    pallas_call x1, Pallas kernels: 141 us -> 138 us  [layer(): pl.pallas_call(layer_kernel, out_shape=(jax.ShapeDtypeStruct((rows, width...]
where the time goes in v6:
time: 144 us; the launch traced here: 143 us
  Pallas kernels  138 us (96%)
  local copies, waits for them, and re-layouts  4.53 us (3%)
    pallas_call x1, Pallas kernels, layer(): pl.pallas_call(layer_kernel, out_shape=(jax.ShapeDtypeStruct((rows, width...  138 us
    unnamed x8, local copies, waits for them, and re-layouts  3.34 us

profile of v6, /device:TPU:1, one launch (start us, length us, event | category | flops | bytes accessed | tf_op | source)
XLA Modules:
  0.0 143.1 jit_solution(3120638628440140879)
XLA Ops:
  0.6 0.0 copy-start.1
  0.6 0.7 copy-done.1
  1.3 0.0 copy-start.2
  1.3 0.6 broadcast_in_dim.6.gain_ref
  1.9 0.1 copy-done.2
  2.0 0.6 broadcast_in_dim.7.feed_gain_ref
  2.6 137.9 %layer_kernel.1 = (bf16[128,1536]{1,0:T(8,128)(2,1)}, bf16[2,48,2048]{2,1,0:T(8,128)(2,1)}) custom-call(s32[32]{0:T(128)} %lengths.1, s32[32]{0:T(128)} %member.1, s32[8]{0:T(128)} %owners.1, bf16[2,48,4096]{2,1,0:T(8,128)(2,1)} %bitcast.7, bf16[128,1536]{1,0:T(8,128)(2,1)} %tok_in.1, bf16[192,96]{1,0:T(8,128)(2,1)} %wq_in.1, bf16[48,192]{1,0:T(8,128)(2,1)} %bitcast.10, ...), custom_call_target="tpu_custom_call" | custom-call | tf_op jit(solution)/shard_map/layer_kernel/pallas_call | solution.py:625
  140.5 0.0 copy-start
  140.5 1.8 %copy.20 = bf16[128,1536]{1,0:T(8,128)(2,1)} copy(bf16[128,1536]{1,0:T(8,128)(2,1)} %get-tuple-element.8) | data formatting | bytes 786432
  142.3 0.0 copy-done
  142.3 0.7 copy.21
Async XLA Ops:
  0.6 0.7 copy-start.1
  1.3 0.7 copy-start.2
  140.5 1.8 %copy-start = (bf16[2,48,2048]{2,1,0:T(8,128)(2,1)S(1)}, bf16[2,48,2048]{2,1,0:T(8,128)(2,1)}, u32[]{:S(2)}) copy-start(bf16[2,48,2048]{2,1,0:T(8,128)(2,1)} %get-tuple-element.5) | copy-start | bytes 1179652

commit v7 on v6

--- a/solution.py
+++ b/solution.py
@@ -543,6 +543,7 @@
                 preferred_element_type=jnp.float32,
             )
             active.append((gate / (1.0 + jnp.exp(-gate)) * lift).astype(jnp.bfloat16))
+        copies = []
         for u in range(4):
             parts = [
                 lax.dot_general(
@@ -556,11 +557,22 @@
             part[slot, :, :, 384 * u : 384 * u + 384] = (
                 (parts[0] + parts[1]).astype(jnp.bfloat16).reshape(2, 128, 384)
             )
-        return go(part.at[slot, 1 - core], from_pair.at[slot], peer(0, True))
-
-    def pair_sum(slot, copy):
-        copy.wait_recv()
-        sums[slot] = part[slot, core].astype(jnp.float32) + from_pair[slot].astype(jnp.float32)
+            if u % 2:
+                side = pl.ds(384 * (u - 1), 768)
+                copies.append(
+                    go(part.at[slot, 1 - core, :, side], from_pair.at[slot, :, side], partner)
+                )
+        return copies
+
+    sides = [slice(768 * k, 768 * k + 768) for k in range(2)]
+
+    def pair_sum(slot, copies, which=(0, 1)):
+        for k in which:
+            copies[k].wait_recv()
+            side = sides[k]
+            sums[slot, :, side] = part[slot, core, :, side].astype(jnp.float32) + from_pair[
+                slot, :, side
+            ].astype(jnp.float32)
 
     across.wait_recv()
     pair0 = feed(0, 0)
@@ -583,21 +595,31 @@
     pair_sum(1, pair1)
     plain[1] = sums[1, 64:128].astype(jnp.bfloat16)
     plain_b = go(plain.at[1], plain.at[3], peer(1))
-    pair_sum(2, pair2)
-    to_relay[...] = sums[2].astype(jnp.bfloat16)
-    relay_a = go(to_relay.at[pl.ds(0, 64)], relay.at[0], peer(1))
-    relay_b = go(to_relay.at[pl.ds(64, 64)], relay.at[1], peer(3))
+    relays = []
+    for k, side in enumerate(sides):
+        pair_sum(2, pair2, (k,))
+        to_relay[:, side] = sums[2, :, side].astype(jnp.bfloat16)
+        cols = pl.ds(768 * k, 768)
+        relays.append(
+            (
+                go(to_relay.at[pl.ds(0, 64), cols], relay.at[0, :, cols], peer(1)),
+                go(to_relay.at[pl.ds(64, 64), cols], relay.at[1, :, cols], peer(3)),
+            )
+        )
     pair_sum(0, pair0)
-    relay_a.wait_recv()
-    joined[0] = (sums[1, 0:64] + relay[0].astype(jnp.float32)).astype(jnp.bfloat16)
-    joined_a = go(joined.at[0], joined.at[2], peer(1))
-    relay_b.wait_recv()
-    joined[1] = (sums[3, 64:128] + relay[1].astype(jnp.float32)).astype(jnp.bfloat16)
-    joined_b = go(joined.at[1], joined.at[3], peer(3))
+    joins = []
+    for k, side in enumerate(sides):
+        cols = pl.ds(768 * k, 768)
+        for h, (slot, du) in enumerate(((1, 1), (3, 3))):
+            relays[k][h].wait_recv()
+            joined[h, :, side] = (
+                sums[slot, 64 * h : 64 * h + 64, side] + relay[h, :, side].astype(jnp.float32)
+            ).astype(jnp.bfloat16)
+            joins.append(go(joined.at[h, :, cols], joined.at[2 + h, :, cols], peer(du)))
     plain_a.wait_recv()
     plain_b.wait_recv()
-    joined_a.wait_recv()
-    joined_b.wait_recv()
+    for copy in joins:
+        copy.wait_recv()
     for h in range(2):
         here = slice(64 * h, 64 * h + 64)
         feed_sum = (

time: 144 us -> 143 us (level)
  no operation moved by 1% of the time
where the time goes in v7:
time: 143 us
  Pallas kernels  138 us (97%)
  local copies, waits for them, and re-layouts  4.53 us (3%)
    pallas_call x1, Pallas kernels, layer(): pl.pallas_call(layer_kernel, out_shape=(jax.ShapeDtypeStruct((rows, width...  138 us
    unnamed x8, local copies, waits for them, and re-layouts  3.34 us

profile of v7, /device:TPU:1, one launch (start us, length us, event | category | flops | bytes accessed | tf_op | source)
XLA Modules:
  0.0 142.7 jit_solution(9988862467475401887)
XLA Ops:
  0.6 0.0 copy-start.1
  0.6 0.7 copy-done.1
  1.3 0.0 copy-start.2
  1.3 0.6 broadcast_in_dim.6.gain_ref
  1.9 0.1 copy-done.2
  2.0 0.6 broadcast_in_dim.7.feed_gain_ref
  2.6 137.5 %layer_kernel.1 = (bf16[128,1536]{1,0:T(8,128)(2,1)}, bf16[2,48,2048]{2,1,0:T(8,128)(2,1)}) custom-call(s32[32]{0:T(128)} %lengths.1, s32[32]{0:T(128)} %member.1, s32[8]{0:T(128)} %owners.1, bf16[2,48,4096]{2,1,0:T(8,128)(2,1)} %bitcast.7, bf16[128,1536]{1,0:T(8,128)(2,1)} %tok_in.1, bf16[192,96]{1,0:T(8,128)(2,1)} %wq_in.1, bf16[48,192]{1,0:T(8,128)(2,1)} %bitcast.10, ...), custom_call_target="tpu_custom_call" | custom-call | tf_op jit(solution)/shard_map/layer_kernel/pallas_call | solution.py:647
  140.1 0.0 copy-start
  140.2 1.8 %copy.20 = bf16[128,1536]{1,0:T(8,128)(2,1)} copy(bf16[128,1536]{1,0:T(8,128)(2,1)} %get-tuple-element.8) | data formatting | bytes 786432
  142.0 0.0 copy-done
  142.0 0.7 copy.21
Async XLA Ops:
  0.6 0.7 copy-start.1
  1.3 0.7 copy-start.2
  140.1 1.8 %copy-start = (bf16[2,48,2048]{2,1,0:T(8,128)(2,1)S(1)}, bf16[2,48,2048]{2,1,0:T(8,128)(2,1)}, u32[]{:S(2)}) copy-start(bf16[2,48,2048]{2,1,0:T(8,128)(2,1)} %get-tuple-element.5) | copy-start | bytes 1179652
